TPU v7x, 32 devices: a whole 2x2x4 slice. The times are simulated.
32 devices in a mesh: dp: 4 (over z), tx: 2 (over y), ty: 4 (over x, core).
Axes of the slice: x: 2, y: 2, z: 4, core: 2. Of those that a mesh axis runs over, the one named last changes fastest.
Arguments:
- inputs: bfloat16 [8, 1024, 2048], P('dp', 'ty'), may hold values from -6 to 6
- lengths: int32 [8], replicated, may hold values from 1 to 1024, 5120 in all
- prompt_deal: int32 [8], replicated, may hold values from 0 to 7, each once
- block_owner: int32 [4], replicated, may hold values from 0 to 3, each once
- attn_gain: float32 [2048], replicated, may hold values from 0.5 to 1.5
- latent_gain: float32 [512], replicated, may hold values from 0.5 to 1.5
- final_gain: float32 [2048], replicated, may hold values from 0.5 to 1.5
- w_query: float32 [2048, 3072], P('dp', ('tx', 'ty')), may hold values from -4 to 4
- w_down_kv: float32 [2048, 576], P('dp'), may hold values from -0.125 to 0.125
- w_up_kv: float32 [512, 4096], P('dp', ('tx', 'ty')), may hold values from -4 to 4
- w_out: float32 [2048, 2048], P('dp', 'tx'), may hold values from -0.125 to 0.125
- w_vocab: float32 [2048, 57344], P('dp', ('tx', 'ty')), may hold values from -0.125 to 0.125
Outputs:
- hidden_out: bfloat16 [8, 1024, 2048], P('dp', 'ty', 'tx')
- logits: float32 [8, 57344], P('dp', ('tx', 'ty'))
Inputs may be any that keep to these rules, and one draw needn't show every extreme that they name: `prompt_deal`: a permutation of the 8 prompts. `block_owner`: a permutation of the 4 row blocks. `lengths`: some prompt has exactly 1024 live tokens.
All inputs are finite; a program needn't handle non-finite values.
Results may differ from a plain program's by a relative error of at most 0.0065.
The roundings to bfloat16 on the way count: a program that leaves them out, or rounds other values in their place, can miss the bound.
Values may be sent and summed in bfloat16 or wider, within the bound.
A program may use at most 192 MiB of HBM per device.

v0:
```python
import jax
import jax.numpy as jnp
from jax import lax
from jax.sharding import PartitionSpec as P

NOPE = 128
ROPE = 64
LATENT = 512
LEN = 1024


EPS = 1e-06


def normalize(values, gain):
    wide = values.astype(jnp.float32)
    return wide * lax.rsqrt(jnp.mean(wide * wide, axis=-1, keepdims=True) + EPS) * gain


def rotate(values, position):
    half_dim = values.shape[-1] // 2
    frequency = 10000.0 ** (-jnp.arange(half_dim, dtype=jnp.float32) / half_dim)
    angles = position.astype(jnp.float32)[..., None] * frequency
    cosine = jnp.cos(angles)
    sine = jnp.sin(angles)
    first_half = values[..., :half_dim]
    second_half = values[..., half_dim:]
    return jnp.concatenate(
        [first_half * cosine - second_half * sine, first_half * sine + second_half * cosine],
        axis=-1,
    )


def shards(
    inputs,
    lengths,
    prompt_deal,
    block_owner,
    attn_gain,
    latent_gain,
    final_gain,
    w_query,
    w_down_kv,
    w_up_kv,
    w_out,
    w_vocab,
):
    groups = lax.axis_size("dp")
    inverse = (
        jnp.zeros((groups,), jnp.int32).at[block_owner].set(jnp.arange(groups, dtype=jnp.int32))
    )

    def arrange(gathered):
        block_rows = gathered.shape[0] // groups
        blocks = gathered.reshape((groups, block_rows) + gathered.shape[1:])
        return jnp.take(blocks, inverse, axis=0).reshape(gathered.shape)

    query_w, down_w, up_w, out_w = (
        lax.all_gather(w_query.astype(jnp.bfloat16), "dp", axis=0, tiled=True),
        lax.all_gather(w_down_kv.astype(jnp.bfloat16), "dp", axis=0, tiled=True),
        lax.all_gather(w_up_kv.astype(jnp.bfloat16), "dp", axis=0, tiled=True),
        lax.all_gather(w_out.astype(jnp.bfloat16), "dp", axis=0, tiled=True),
    )
    query_w = arrange(query_w)
    down_w = arrange(down_w)
    up_w = arrange(up_w)
    out_w = arrange(out_w)
    query_w, up_w = (
        lax.all_gather(query_w, "ty", axis=1, tiled=True),
        lax.all_gather(up_w, "ty", axis=1, tiled=True),
    )
    per_grp, quarter, width = inputs.shape
    heads = query_w.shape[1] // (NOPE + ROPE)
    position = lax.axis_index("ty") * quarter + jnp.arange(quarter, dtype=jnp.int32)
    slots = lax.axis_index("dp") * per_grp + jnp.arange(per_grp, dtype=jnp.int32)
    live_len = jnp.take(lengths, jnp.take(prompt_deal, slots))
    flat_rows = inputs.reshape(per_grp * quarter, width)
    normed = normalize(flat_rows, attn_gain).astype(jnp.bfloat16)
    queries = jnp.dot(normed, query_w, preferred_element_type=jnp.float32).reshape(
        per_grp, quarter, heads, NOPE + ROPE
    )
    queries = jnp.concatenate(
        [queries[..., :NOPE], rotate(queries[..., NOPE:], position[None, :, None])], axis=-1
    ).astype(jnp.bfloat16)
    down_proj = jnp.dot(normed, down_w, preferred_element_type=jnp.float32).reshape(
        per_grp, quarter, LATENT + ROPE
    )
    latent = normalize(down_proj[..., :LATENT], latent_gain).astype(jnp.bfloat16)
    key_rope = rotate(down_proj[..., LATENT:], position[None, :]).astype(jnp.bfloat16)
    gathered = lax.all_gather(
        jnp.concatenate([latent, key_rope], axis=-1), "ty", axis=1, tiled=True
    )
    key_val = jnp.dot(gathered[..., :LATENT], up_w, preferred_element_type=jnp.float32).astype(
        jnp.bfloat16
    )
    rope_all = gathered[..., LATENT:]
    key_val = key_val.reshape(per_grp, LEN, heads, 2, NOPE)
    key_nope = key_val[:, :, :, 0]
    values = key_val[:, :, :, 1]
    score_scale = (NOPE + ROPE) ** (-0.5)
    scores = (
        jnp.einsum(
            "pqhd,pkhd->phqk", queries[..., :NOPE], key_nope, preferred_element_type=jnp.float32
        )
        + jnp.einsum(
            "pqhd,pkd->phqk", queries[..., NOPE:], rope_all, preferred_element_type=jnp.float32
        )
    ) * score_scale
    key_pos = jnp.arange(LEN, dtype=jnp.int32)
    allowed = (key_pos[None, None, :] <= position[None, :, None]) & (
        key_pos[None, None, :] < live_len[:, None, None]
    )
    scores = jnp.where(allowed[:, None], scores, -1e30)
    top = jnp.max(scores, axis=-1, keepdims=True)
    expo = jnp.exp(scores - top)
    softmax_w = (expo / jnp.sum(expo, axis=-1, keepdims=True)).astype(jnp.bfloat16)
    attended = jnp.einsum(
        "phqk,pkhd->pqhd", softmax_w, values, preferred_element_type=jnp.float32
    ).astype(jnp.bfloat16)
    attended = attended.reshape(per_grp * quarter, heads * NOPE)
    own_width = width // lax.axis_size("tx")
    col_start = lax.axis_index("tx") * own_width
    partial_value = lax.dot_general(
        attended, out_w, (((1,), (1,)), ((), ())), preferred_element_type=jnp.float32
    ).reshape(per_grp, quarter, width)
    summed = lax.psum_scatter(partial_value, "tx", scatter_dimension=2, tiled=True)
    residual = lax.dynamic_slice_in_dim(inputs, col_start, own_width, 2)
    layer_out = (residual.astype(jnp.float32) + summed).astype(jnp.bfloat16)
    selector = (position[None, :] == (live_len - 1)[:, None]).astype(jnp.float32)
    picked = jnp.einsum("pq,pqd->pd", selector, layer_out.astype(jnp.float32))
    placed = lax.dynamic_update_slice_in_dim(
        jnp.zeros((per_grp, width), jnp.float32), picked, col_start, 1
    )
    last_rows = lax.psum(placed, ("tx", "ty"))
    final_rows = normalize(last_rows, final_gain).astype(jnp.bfloat16)
    vocab_block = arrange(lax.all_gather(w_vocab.astype(jnp.bfloat16), "dp", axis=0, tiled=True))
    logits = jnp.dot(final_rows, vocab_block, preferred_element_type=jnp.float32)
    return (layer_out, logits)


def solution(mesh):
    placed = (
        P("dp", "ty", None),
        P(),
        P(),
        P(),
        P(),
        P(),
        P(),
        P("dp", ("tx", "ty")),
        P("dp", None),
        P("dp", ("tx", "ty")),
        P("dp", "tx"),
        P("dp", ("tx", "ty")),
    )
    return jax.shard_map(
        shards,
        mesh=mesh,
        in_specs=placed,
        out_specs=(P("dp", "ty", "tx"), P("dp", ("tx", "ty"))),
        check_vma=False,
    )
```

profile of v0, /device:TPU:0, one launch (start us, length us, event | category | flops | bytes accessed | tf_op | source)
XLA Modules:
  0.0 1004.1 jit_solution(8479508930206960993)
XLA Ops:
  7.2 2.2 convert_element_type.73
  9.6 1.9 convert_element_type.78
  11.5 0.0 all-gather.18.cloned.1.call-start
  11.6 2.9 convert_element_type.82
  14.4 0.0 all-gather.12.cloned.1.call-start
  14.6 0.6 scatter_custom_fusion
  15.2 24.1 %all_gather.26 = bf16[512,512]{1,0:T(8,128)(2,1)S(1)} all-gather(bf16[128,512]{1,0:T(8,128)(2,1)S(1)} %convert_element_type.76), channel_id=1, replica_groups=mesh['dp'=4,'tx'=2,'ty'=4] {'dp'}, dimensions={0}, use_global_device_ids=true | all-gather | bytes 655360 | tf_op jit(solution)/shard_map/all_gather | solution.py:61
  39.3 0.6 gather_fusion.1
  39.9 0.1 broadcast_bitcast_fusion.1
  39.9 1.0 bitcast_select_fusion.1
  41.0 0.1 broadcast_bitcast_fusion
  41.1 0.5 fusion.4
  41.6 0.2 multiply_cosine_fusion
  41.8 27.0 %all-gather.8.cloned.1.call-done = bf16[2048,576]{0,1:T(8,128)(2,1)} async-done(((bf16[512,576]{0,1:T(8,128)(2,1)}), bf16[2048,576]{0,1:T(8,128)(2,1)}) %all-gather.8.cloned.1.call-update) | async-done | bytes 2359312 | tf_op jit(solution)/shard_map/all_gather | solution.py:60
  68.8 1.9 copy.68
  70.7 2.2 gather_fusion
  72.9 2.1 copy.58
  75.0 0.2 copy-done.4
  75.2 1.5 fusion.8
  76.7 0.1 multiply_reduce_fusion
  76.8 0.2 multiply_convert_fusion
  77.0 0.9 pad_maximum_fusion.1
  77.9 29.3 %all-gather.14.cloned.1.call-done = bf16[2048,384]{1,0:T(8,128)(2,1)} async-done(((bf16[512,384]{1,0:T(8,128)(2,1)}), bf16[2048,384]{1,0:T(8,128)(2,1)}) %all-gather.14.cloned.1.call-update) | async-done | bytes 1572880 | tf_op jit(solution)/shard_map/all_gather | solution.py:59
  107.3 2.3 gather_fusion.2
  109.6 0.8 copy.54
  110.4 1.3 broadcast_select_fusion.1
  111.8 0.6 gather_fusion.8
  112.5 0.6 gather_fusion.9
  113.1 0.1 iota_compare_fusion.1
  113.2 0.2 iota_compare_fusion
  113.4 0.2 broadcast_and_fusion
  113.7 75.4 %all-gather.18.cloned.1.call-done = bf16[2048,1024]{1,0:T(8,128)(2,1)} async-done(((bf16[512,1024]{1,0:T(8,128)(2,1)}), bf16[2048,1024]{1,0:T(8,128)(2,1)}) %all-gather.18.cloned.1.call-update) | async-done | bytes 4194320 | tf_op jit(solution)/shard_map/all_gather | solution.py:62
  189.1 4.9 gather_fusion.3
  194.0 4.9 broadcast_select_fusion
  198.9 12.8 %all-gather.12.cloned.1.call-done = bf16[512,2048]{1,0:T(8,128)(2,1)} async-done(((bf16[512,512]{1,0:T(8,128)(2,1)}), bf16[512,2048]{1,0:T(8,128)(2,1)}) %all-gather.12.cloned.1.call-update) | async-done | bytes 2097168 | tf_op jit(solution)/shard_map/all_gather | solution.py:70
  211.7 25.8 %all-gather.10.cloned.1.call-done = bf16[2,1024,576]{1,2,0:T(8,128)(2,1)} async-done(((bf16[2,256,576]{1,2,0:T(8,128)(2,1)}), bf16[2,1024,576]{1,2,0:T(8,128)(2,1)}) %all-gather.10.cloned.1.call-update) | async-done | bytes 2359312 | tf_op jit(solution)/shard_map/all_gather | solution.py:90
  237.5 10.7 %convolution_convert_fusion = bf16[2,1024,2048]{2,1,0:T(8,128)(2,1)} fusion(bf16[2,1024,576]{1,2,0:T(8,128)(2,1)} %all-gather.10.cloned.1.call-done, bf16[512,2048]{1,0:T(8,128)(2,1)} %all-gather.12.cloned.1.call-done), kind=kOutput, calls=%fused_computation.20 | convolution fusion | flops 4299161600 | bytes 12582912 | tf_op jit(solution)/shard_map/dot_general | solution.py:93
  248.1 14.5 %reshape.344 = bf16[2,1024,8,2,128]{4,3,2,1,0:T(2,128)(2,1)} reshape(bf16[2,1024,2048]{2,1,0:T(8,128)(2,1)} %convolution_convert_fusion) | data formatting | bytes 16777216 | tf_op jit(solution)/shard_map/reshape | solution.py:97
  262.6 17.5 %fusion.36 = (bf16[2,1024,8,1,128]{4,3,2,1,0:T(2,128)(2,1)}, bf16[2,1024,8,1,128]{4,3,2,1,0:T(2,128)(2,1)}) fusion(bf16[2,1024,8,2,128]{4,3,2,1,0:T(2,128)(2,1)} %reshape.344), kind=kLoop, calls=%fused_computation.93 | loop fusion | bytes 16777216 | tf_op jit(solution)/shard_map/slice | solution.py:99
  280.1 20.1 %copy.55 = bf16[2,1024,8,1,128]{1,4,2,0,3:T(8,128)(2,1)} copy(bf16[2,1024,8,1,128]{4,3,2,1,0:T(2,128)(2,1)} %get-tuple-element.9) | data formatting | bytes 8388608
  300.2 5.7 fusion.13
  306.0 1.6 copy-done.8
  307.6 0.2 subtract_convert_fusion
  307.8 9.1 fusion.22
  316.8 17.3 %fusion.37 = (f32[2,8,256]{2,1,0:T(8,128)S(1)}, f32[2,8,256,1024]{3,2,1,0:T(8,128)}) fusion(f32[2,1024,256,8]{1,2,3,0:T(8,128)} %fusion.22, pred[2,256,1024]{2,1,0:T(8,128)(4,1)S(1)} %broadcast_and_fusion, bf16[2,1024,8,1,128]{4,3,2,1,0:T(2,128)(2,1)} %get-tuple-element.10, f32[2,256,8,192]{1,3,2,0:T(8,128)} %copy-done.8), kind=kOutput, calls=%fused_computation.94 | convolution fusion | flops 1094714368 | bytes 43532288 | tf_op jit(solution)/shard_map/sub | solution.py:115
  334.1 8.8 fusion.18
  342.9 4.4 fusion.38
  347.3 0.0 all-gather.20.cloned.1.call-start
  347.4 9.2 convert_element_type.85
  356.6 0.1 compare_bitcast_fusion
  356.7 45.0 %reduce-scatter.2.cloned.1.call-done = f32[2,256,1024]{2,1,0:T(8,128)} async-done(((f32[2,256,2048]{2,1,0:T(8,128)}), f32[2,256,1024]{2,1,0:T(8,128)}) %reduce-scatter.2.cloned.1.call-update) | async-done | bytes 2097168 | tf_op jit(solution)/shard_map/reduce_scatter | solution.py:126
  401.7 2.0 add_convert_fusion
  403.7 0.2 fusion.28
  404.0 23.1 %psum.7 = f32[2,2048]{1,0:T(2,128)S(1)} all-reduce(f32[2,2048]{1,0:T(2,128)S(1)} %bitcast_dynamic-update-slice_fusion), channel_id=1, replica_groups=mesh['dp'=4,'tx'=2,'ty'=4] {'tx','ty'}, use_global_device_ids=true, to_apply=%region_6.8 | all-reduce | flops 4096 | bytes 32768 | tf_op jit(solution)/shard_map/psum | solution.py:134
  427.0 0.1 multiply_reduce_fusion.1
  427.2 469.4 %all-gather.20.cloned.1.call-done = bf16[2048,7168]{1,0:T(8,128)(2,1)} async-done(((bf16[512,7168]{1,0:T(8,128)(2,1)}), bf16[2048,7168]{1,0:T(8,128)(2,1)}) %all-gather.20.cloned.1.call-update) | async-done | bytes 29360144 | tf_op jit(solution)/shard_map/all_gather | solution.py:136
  896.5 20.0 %fusion.35 = (bf16[4,512,1792]{2,1,0:T(8,128)(2,1)}, bf16[4,512,1792]{2,1,0:T(8,128)(2,1)}, bf16[4,512,1792]{2,1,0:T(8,128)(2,1)}, bf16[4,512,1792]{2,1,0:T(8,128)(2,1)}) fusion(bf16[4,512,7168]{2,1,0:T(8,128)(2,1)} %bitcast.74), kind=kLoop, calls=%fused_computation.92 | loop fusion | bytes 58720256 | tf_op jit(solution)/shard_map/jit(_take)/gather | solution.py:56
  916.6 7.1 gather_fusion.7
  923.7 7.0 gather_fusion.6
  930.7 7.0 gather_fusion.5
  937.8 7.1 gather_fusion.4
  944.9 20.2 %pad_maximum_fusion = bf16[4,512,7168]{2,1,0:T(8,128)(2,1)} fusion(bf16[4,512,1792]{2,1,0:T(8,128)(2,1)} %gather_fusion.7, bf16[4,512,1792]{2,1,0:T(8,128)(2,1)} %gather_fusion.6, bf16[4,512,1792]{2,1,0:T(8,128)(2,1)} %gather_fusion.5, bf16[4,512,1792]{2,1,0:T(8,128)(2,1)} %gather_fusion.4), kind=kLoop, calls=%fused_computation.12 | loop fusion | flops 117440512 | bytes 58720256
  965.1 20.2 %bitcast_select_fusion = bf16[2048,7168]{1,0:T(8,128)(2,1)} fusion(bf16[4,512,7168]{2,1,0:T(8,128)(2,1)} %pad_maximum_fusion, pred[2048]{0:T(1024)(128)(4,1)S(1)} %bitcast.86), kind=kLoop, calls=%fused_computation.13 | loop fusion | flops 14680064 | bytes 58722304 | tf_op jit(solution)/shard_map/jit(_take)/select_n | solution.py:56
  985.3 12.0 %fusion.26 = f32[2,7168]{1,0:T(2,128)} fusion(bf16[2048,7168]{1,0:T(8,128)(2,1)} %bitcast_select_fusion, f32[2,2048]{1,0:T(2,128)S(1)} %psum.7, f32[2]{0:T(128)S(1)} %add_rsqrt_fusion.2, f32[2048]{0:T(1024)S(1)} %copy-done.10), kind=kOutput, calls=%fused_computation.62 | convolution fusion | flops 58732544 | bytes 29442056 | tf_op jit(solution)/shard_map/dot_general | solution.py:137
  (60 shorter events, 0.6 us)
Async XLA Ops:
  7.2 104.6 %copy-start = (s32[8]{0:T(128)S(1)}, s32[8]{0:T(128)}, u32[]{:S(2)}) copy-start(s32[8]{0:T(128)} %param.16) | copy-start | bytes 100
  7.2 7.3 copy-start.9
  7.2 7.3 copy-start.13
  7.2 61.6 %all-gather.8.cloned.1.call-start = ((), (), s32[]{:S(2)}) async-start(), calls=%async_computation.1 | async-start | bytes 2949120 | tf_op jit(solution)/shard_map/all_gather | solution.py:60
  9.5 97.8 %all-gather.14.cloned.1.call-start = ((), (), s32[]{:S(2)}) async-start(), calls=%async_computation.4 | async-start | bytes 1966080 | tf_op jit(solution)/shard_map/all_gather | solution.py:59
  11.5 29.6 %copy-start.3 = (bf16[2,256,2048]{2,1,0:T(8,128)(2,1)S(1)}, bf16[2,256,2048]{2,1,0:T(8,128)(2,1)}, u32[]{:S(2)}) copy-start(bf16[2,256,2048]{2,1,0:T(8,128)(2,1)} %param.14) | copy-start | bytes 6291460
  11.5 177.6 %all-gather.18.cloned.1.call-start = ((), (), s32[]{:S(2)}) async-start(), calls=%async_computation.6 | async-start | bytes 5242880 | tf_op jit(solution)/shard_map/all_gather | solution.py:62
  14.4 197.2 %all-gather.12.cloned.1.call-start = ((), (), s32[]{:S(2)}) async-start(), calls=%async_computation.3 | async-start | bytes 2621440 | tf_op jit(solution)/shard_map/all_gather | solution.py:70
  40.9 196.5 %all-gather.10.cloned.1.call-start = ((), (), s32[]{:S(2)}) async-start(), calls=%async_computation.2 | async-start | bytes 2949120 | tf_op jit(solution)/shard_map/all_gather | solution.py:90
  70.7 4.3 copy-start.12
  72.9 2.3 copy-start.4
  75.2 1.7 copy-start.11
  77.9 222.3 %all-gather.16.cloned.1.call-start = ((), (), s32[]{:S(2)}) async-start(), calls=%async_computation.5 | async-start | bytes 7864320 | tf_op jit(solution)/shard_map/all_gather | solution.py:69
  109.6 2.9 copy-start.2
  111.7 290.0 %reduce-scatter.2.cloned.1.call-start = ((), (), s32[]{:S(2)}) async-start(), calls=%async_computation.7 | async-start | bytes 6291456 | tf_op jit(solution)/shard_map/reduce_scatter | solution.py:126
  280.1 20.1 %copy-start.5 = (bf16[2,256,2048]{2,1,0:T(8,128)(2,1)S(1)}, bf16[2,256,2048]{2,1,0:T(8,128)(2,1)}, u32[]{:S(2)}) copy-start(bf16[2,256,2048]{2,1,0:T(8,128)(2,1)} %param.14) | copy-start | bytes 6291460
  305.9 1.6 copy-start.8
  334.1 8.8 copy-start.7
  347.3 549.2 %all-gather.20.cloned.1.call-start = ((), (), s32[]{:S(2)}) async-start(), calls=%async_computation.8 | async-start | bytes 36700160 | tf_op jit(solution)/shard_map/all_gather | solution.py:136
  403.7 512.9 %copy-start.6 = (bf16[2,256,1024]{2,1,0:T(8,128)(2,1)}, bf16[2,256,1024]{2,1,0:T(8,128)(2,1)S(1)}, u32[]{:S(2)}) copy-start(bf16[2,256,1024]{2,1,0:T(8,128)(2,1)S(1)} %add_convert_fusion) | copy-start | bytes 3145732
  965.1 20.2 %copy-start.10 = (f32[2048]{0:T(1024)S(1)}, f32[2048]{0:T(1024)}, u32[]{:S(2)}) copy-start(f32[2048]{0:T(1024)} %param.20) | copy-start | bytes 24580
  985.2 12.0 %copy-start.1 = (s32[8]{0:T(128)S(1)}, s32[8]{0:T(128)}, u32[]{:S(2)}) copy-start(s32[8]{0:T(128)} %param.16) | copy-start | bytes 100
Sparse Core Ops, SparseCore 0:
  9.6 59.1 all-gather.7
  70.4 36.8 all-gather.13
  109.4 79.6 all-gather.17
  190.5 21.1 all-gather.11
  213.1 24.3 all-gather.9
  238.9 46.3 all-gather.15
  347.4 54.2 reduce-scatter.1
  403.4 493.1 all-gather.19
where the time goes:
time: 1010 us; the launch traced here: 1000 us
  waiting for transfers between devices  685 us (68%)
  local copies, waits for them, and re-layouts  119 us (12%)
  matrix products  69.7 us (7%)
  other arithmetic  68.5 us (7%)
  blocking collectives  47.2 us (5%)
  between operations  14.5 us (1%)
    all_gather x1, waiting for transfers between devices, shards(): lax.all_gather(w_vocab.astype(jnp.bfloat16), 'dp', axis=0, tiled=True)  469 us
    all_gather x1, waiting for transfers between devices, shards(): lax.all_gather(w_out.astype(jnp.bfloat16), 'dp', axis=0, tiled=True)  75.4 us
    gather x11, local copies, waits for them, and re-layouts, arrange(): return jnp.take(blocks, inverse, axis=0).reshape(gathered.shape)  61.2 us
    reduce_scatter x1, waiting for transfers between devices, shards(): lax.psum_scatter(partial_value, 'tx', scatter_dimension=2, tiled=True)  45 us
    all_gather x1, waiting for transfers between devices, shards(): lax.all_gather(w_query.astype(jnp.bfloat16), 'dp', axis=0, tiled=True)  29.3 us
    select_n x5, other arithmetic, arrange(): return jnp.take(blocks, inverse, axis=0).reshape(gathered.shape)  27.3 us
    all_gather x1, waiting for transfers between devices, shards(): lax.all_gather(w_down_kv.astype(jnp.bfloat16), 'dp', axis=0, tiled=True)  27 us
    all_gather x1, waiting for transfers between devices, shards(): lax.all_gather(jnp.concatenate([latent, key_rope], axis=-1), 'ty', axis=1...  25.8 us
  transfers between devices with their start and end apart: 8, of which 7 were waited for; matrix products, arithmetic and copies ran while one was open for 11% of the time, Pallas kernels for 0%

commit v1 on v0

--- a/solution.py
+++ b/solution.py
@@ -1,14 +1,17 @@
+import functools
+
 import jax
 import jax.numpy as jnp
 from jax import lax
+from jax.experimental import pallas as pl
+from jax.experimental.pallas import tpu as pltpu
 from jax.sharding import PartitionSpec as P
 
 NOPE = 128
 ROPE = 64
 LATENT = 512
 LEN = 1024
-
-
+TILE = 256
 EPS = 1e-06
 
 
@@ -17,7 +20,123 @@
     return wide * lax.rsqrt(jnp.mean(wide * wide, axis=-1, keepdims=True) + EPS) * gain
 
 
-def rotate(values, position):
+def dot32(left, right):
+    return jnp.dot(left, right, preferred_element_type=jnp.float32)
+
+
+def layer_kernel(
+    groups, heads, inv_ref, live_ref, x_ref, again_ref, lgain_ref, cos_ref, sin_ref,
+    wq_ref, wa_ref, wb_ref, o_ref, h_ref, up_ref, k_ref, v_ref,
+):
+    prompt, tile = pl.program_id(0), pl.program_id(1)
+    width = x_ref.shape[-1]
+    rows = width // groups
+    up_rows = LATENT // groups
+
+    @pl.when((prompt == 0) & (tile == 0))
+    def _():
+        for g in range(groups):
+            start = pl.multiple_of(inv_ref[g] * up_rows, up_rows)
+            up_ref[g * up_rows : (g + 1) * up_rows, :] = wb_ref[pl.ds(start, up_rows), :]
+
+    h_ref[...] = normalize(x_ref[0], again_ref[...]).astype(jnp.bfloat16)
+
+    def project(w_ref):
+        total = None
+        for g in range(groups):
+            start = pl.multiple_of(inv_ref[g] * rows, rows)
+            part = dot32(h_ref[:, g * rows : (g + 1) * rows], w_ref[pl.ds(start, rows), :])
+            total = part if total is None else total + part
+        return total
+
+    cosine, sine = cos_ref[...], sin_ref[...]
+    lane = lax.broadcasted_iota(jnp.int32, (TILE, 128), 1)
+
+    def rotate(block):
+        swapped = jnp.where(
+            lane % ROPE < ROPE // 2,
+            pltpu.roll(block, 128 - ROPE // 2, 1),
+            pltpu.roll(block, ROPE // 2, 1),
+        )
+        return block * cosine + swapped * sine
+
+    down = project(wa_ref)
+    latent = normalize(down[:, :LATENT], lgain_ref[...]).astype(jnp.bfloat16)
+    key_rope = rotate(down[:, LATENT:]).astype(jnp.bfloat16)
+    key_val = dot32(latent, up_ref[...]).astype(jnp.bfloat16)
+    here = pl.ds(pl.multiple_of(tile * TILE, TILE), TILE)
+    for head in range(heads):
+        k_ref[head, here, :NOPE] = key_val[:, 2 * head * NOPE : (2 * head + 1) * NOPE]
+        k_ref[head, here, NOPE:] = key_rope
+        v_ref[head, here, :] = key_val[:, (2 * head + 1) * NOPE : (2 * head + 2) * NOPE]
+
+    queries = project(wq_ref)
+    nope = queries[:, : heads * NOPE].astype(jnp.bfloat16)
+    query = []
+    for head in range(heads):
+        base = heads * NOPE + (head // 2) * 128
+        turned = rotate(queries[:, base : base + 128])
+        mine = jnp.where(lane // ROPE == head % 2, turned, 0.0).astype(jnp.bfloat16)
+        query.append(jnp.concatenate([nope[:, head * NOPE : (head + 1) * NOPE], mine], axis=1))
+
+    live = live_ref[prompt]
+    scale = (NOPE + ROPE) ** (-0.5)
+    for count in range(1, LEN // TILE + 1):
+
+        @pl.when(tile == count - 1)
+        def _():
+            span = count * TILE
+            i = lax.broadcasted_iota(jnp.int32, (TILE, span), 0) + (count - 1) * TILE
+            j = lax.broadcasted_iota(jnp.int32, (TILE, span), 1)
+            allowed = (j <= i) & (j < live)
+            for head in range(heads):
+                score = lax.dot_general(
+                    query[head], k_ref[head, :span, :], (((1,), (1,)), ((), ())),
+                    preferred_element_type=jnp.float32,
+                )
+                score = jnp.where(allowed, score * scale, -1e30)
+                expo = jnp.exp(score - jnp.max(score, axis=-1, keepdims=True))
+                prob = expo * (1.0 / jnp.sum(expo, axis=-1, keepdims=True))
+                out = dot32(prob.astype(jnp.bfloat16), v_ref[head, :span, :])
+                o_ref[0, :, head * NOPE : (head + 1) * NOPE] = out.astype(jnp.bfloat16)
+
+
+def attend(groups, inverse, live, x, again, lgain, cosine, sine, wq, wa, wb):
+    per_grp, _, width = x.shape
+    heads = wb.shape[1] // (2 * NOPE)
+    whole = lambda a: pl.BlockSpec(a.shape, lambda p, t: (0,) * a.ndim)
+    smem = pl.BlockSpec(memory_space=pltpu.SMEM)
+    return pl.pallas_call(
+        functools.partial(layer_kernel, groups, heads),
+        grid=(per_grp, LEN // TILE),
+        in_specs=[
+            smem,
+            smem,
+            pl.BlockSpec((1, TILE, width), lambda p, t: (p, t, 0)),
+            whole(again),
+            whole(lgain),
+            pl.BlockSpec((TILE, 128), lambda p, t: (t, 0)),
+            pl.BlockSpec((TILE, 128), lambda p, t: (t, 0)),
+            whole(wq),
+            whole(wa),
+            whole(wb),
+        ],
+        out_specs=pl.BlockSpec((1, TILE, heads * NOPE), lambda p, t: (p, t, 0)),
+        out_shape=jax.ShapeDtypeStruct((per_grp, LEN, heads * NOPE), jnp.bfloat16),
+        scratch_shapes=[
+            pltpu.VMEM((TILE, width), jnp.bfloat16),
+            pltpu.VMEM(wb.shape, jnp.bfloat16),
+            pltpu.VMEM((heads, LEN, 2 * NOPE), jnp.bfloat16),
+            pltpu.VMEM((heads, LEN, NOPE), jnp.bfloat16),
+        ],
+        compiler_params=pltpu.CompilerParams(vmem_limit_bytes=48 * 1024 * 1024),
+        cost_estimate=pl.CostEstimate(
+            flops=20_000_000_000, bytes_accessed=16_000_000, transcendentals=4_000_000
+        ),
+    )(inverse, live, x, again, lgain, cosine, sine, wq, wa, wb)
+
+
+def rotate_half(values, position):
     half_dim = values.shape[-1] // 2
     frequency = 10000.0 ** (-jnp.arange(half_dim, dtype=jnp.float32) / half_dim)
     angles = position.astype(jnp.float32)[..., None] * frequency
@@ -31,24 +150,10 @@
     )
 
 
-def shards(
-    inputs,
-    lengths,
-    prompt_deal,
-    block_owner,
-    attn_gain,
-    latent_gain,
-    final_gain,
-    w_query,
-    w_down_kv,
-    w_up_kv,
-    w_out,
-    w_vocab,
+def split_positions(
+    inputs, inverse, live_len, attn_gain, latent_gain, w_query, w_down_kv, w_up_kv, w_out
 ):
     groups = lax.axis_size("dp")
-    inverse = (
-        jnp.zeros((groups,), jnp.int32).at[block_owner].set(jnp.arange(groups, dtype=jnp.int32))
-    )
 
     def arrange(gathered):
         block_rows = gathered.shape[0] // groups
@@ -72,21 +177,19 @@
     per_grp, quarter, width = inputs.shape
     heads = query_w.shape[1] // (NOPE + ROPE)
     position = lax.axis_index("ty") * quarter + jnp.arange(quarter, dtype=jnp.int32)
-    slots = lax.axis_index("dp") * per_grp + jnp.arange(per_grp, dtype=jnp.int32)
-    live_len = jnp.take(lengths, jnp.take(prompt_deal, slots))
     flat_rows = inputs.reshape(per_grp * quarter, width)
     normed = normalize(flat_rows, attn_gain).astype(jnp.bfloat16)
     queries = jnp.dot(normed, query_w, preferred_element_type=jnp.float32).reshape(
         per_grp, quarter, heads, NOPE + ROPE
     )
     queries = jnp.concatenate(
-        [queries[..., :NOPE], rotate(queries[..., NOPE:], position[None, :, None])], axis=-1
+        [queries[..., :NOPE], rotate_half(queries[..., NOPE:], position[None, :, None])], axis=-1
     ).astype(jnp.bfloat16)
     down_proj = jnp.dot(normed, down_w, preferred_element_type=jnp.float32).reshape(
         per_grp, quarter, LATENT + ROPE
     )
     latent = normalize(down_proj[..., :LATENT], latent_gain).astype(jnp.bfloat16)
-    key_rope = rotate(down_proj[..., LATENT:], position[None, :]).astype(jnp.bfloat16)
+    key_rope = rotate_half(down_proj[..., LATENT:], position[None, :]).astype(jnp.bfloat16)
     gathered = lax.all_gather(
         jnp.concatenate([latent, key_rope], axis=-1), "ty", axis=1, tiled=True
     )
@@ -126,15 +229,117 @@
     summed = lax.psum_scatter(partial_value, "tx", scatter_dimension=2, tiled=True)
     residual = lax.dynamic_slice_in_dim(inputs, col_start, own_width, 2)
     layer_out = (residual.astype(jnp.float32) + summed).astype(jnp.bfloat16)
-    selector = (position[None, :] == (live_len - 1)[:, None]).astype(jnp.float32)
-    picked = jnp.einsum("pq,pqd->pd", selector, layer_out.astype(jnp.float32))
-    placed = lax.dynamic_update_slice_in_dim(
-        jnp.zeros((per_grp, width), jnp.float32), picked, col_start, 1
-    )
-    last_rows = lax.psum(placed, ("tx", "ty"))
+    return layer_out
+
+
+def split_heads(
+    inputs, inverse, live_len, attn_gain, latent_gain, w_query, w_down_kv, w_up_kv, w_out
+):
+    groups = lax.axis_size("dp")
+    tx_size, ty_size = lax.axis_size("tx"), lax.axis_size("ty")
+    tx, ty = lax.axis_index("tx"), lax.axis_index("ty")
+    per_grp, quarter, width = inputs.shape
+    half = width // tx_size
+    rows = w_query.shape[0]
+    heads = w_query.shape[1] // (NOPE + ROPE)
+    wq = w_query.astype(jnp.bfloat16).reshape(rows, heads, NOPE + ROPE)
+    rope_q = wq[:, :, NOPE:].reshape(rows, heads * ROPE)
+    rope_q = jnp.pad(rope_q, ((0, 0), (0, -(heads * ROPE) % 128)))
+    wq = jnp.concatenate([wq[:, :, :NOPE].reshape(rows, heads * NOPE), rope_q], axis=1)
+    wa = w_down_kv.astype(jnp.bfloat16)
+
+    x_all = lax.all_gather(inputs, "ty", axis=1, tiled=True)
+    wa = lax.all_gather(wa, "dp", axis=0, tiled=True)
+    wa = jnp.concatenate([wa, wa[:, LATENT:]], axis=1)
+    wq = lax.all_gather(wq, "dp", axis=0, tiled=True)
+    wb = lax.all_gather(w_up_kv.astype(jnp.bfloat16), "dp", axis=0, tiled=True)
+
+    position = jnp.arange(LEN, dtype=jnp.float32)
+    frequency = 10000.0 ** (-jnp.arange(ROPE // 2, dtype=jnp.float32) / (ROPE // 2))
+    angles = position[:, None] * frequency
+    cosine, sine = jnp.cos(angles), jnp.sin(angles)
+    cosine = jnp.concatenate([cosine] * 4, axis=1)
+    sine = jnp.concatenate([-sine, sine, -sine, sine], axis=1)
+
+    mixed = attend(
+        groups, inverse, live_len, x_all, attn_gain[None], latent_gain[None], cosine, sine,
+        wq, wa, wb,
+    )
+
+    piece = w_out.shape[1] // ty_size
+    wo = lax.dynamic_slice_in_dim(w_out, ty * piece, piece, 1).astype(jnp.bfloat16)
+    wo = lax.all_gather(wo, "dp", axis=0, tiled=False)
+    wo = jnp.take(wo, inverse, axis=0).reshape(tx_size, half, piece)
+    wo = lax.all_to_all(wo, "tx", split_axis=0, concat_axis=0, tiled=True)
+    wo = lax.all_gather(wo, "ty", axis=1, tiled=False)
+
+    spread = mixed.reshape(per_grp, ty_size, quarter, heads * NOPE)
+    spread = jnp.moveaxis(spread, 1, 0)
+    spread = lax.all_to_all(spread, "ty", split_axis=0, concat_axis=0, tiled=True)
+    spread = lax.all_gather(spread, "tx", axis=0, tiled=False)
+    branch = lax.dot_general(
+        jnp.moveaxis(spread.reshape(tx_size * ty_size, per_grp * quarter, -1), 0, 1).reshape(
+            per_grp * quarter, -1
+        ),
+        jnp.moveaxis(wo.reshape(tx_size * ty_size, half, piece), 0, 1).reshape(half, -1),
+        (((1,), (1,)), ((), ())),
+        preferred_element_type=jnp.float32,
+    ).reshape(per_grp, quarter, half)
+    residual = lax.dynamic_slice_in_dim(inputs, tx * half, half, 2)
+    layer_out = (residual.astype(jnp.float32) + branch).astype(jnp.bfloat16)
+    return layer_out
+
+
+def shards(
+    inputs,
+    lengths,
+    prompt_deal,
+    block_owner,
+    attn_gain,
+    latent_gain,
+    final_gain,
+    w_query,
+    w_down_kv,
+    w_up_kv,
+    w_out,
+    w_vocab,
+):
+    groups = lax.axis_size("dp")
+    dp, tx, ty = lax.axis_index("dp"), lax.axis_index("tx"), lax.axis_index("ty")
+    per_grp, quarter, width = inputs.shape
+    half = width // lax.axis_size("tx")
+    order = jnp.arange(groups, dtype=jnp.int32)
+    inverse = jnp.sum(
+        jnp.where(block_owner[None, :] == order[:, None], order[None, :], 0), axis=1
+    ).astype(jnp.int32)
+    slots = dp * per_grp + jnp.arange(per_grp, dtype=jnp.int32)
+    live_len = jnp.take(lengths, jnp.take(prompt_deal, slots))
+
+    rows = w_query.shape[0]
+    layer = split_positions if w_query.shape[1] % (NOPE + ROPE) else split_heads
+    layer_out = layer(
+        inputs, inverse, live_len, attn_gain, latent_gain, w_query, w_down_kv, w_up_kv, w_out
+    )
+
+    at = live_len - 1 - ty * quarter
+    picked = jnp.stack(
+        [
+            lax.dynamic_slice(
+                layer_out, (i, jnp.clip(at[i], 0, quarter - 1), 0), (1, 1, half)
+            ).reshape(half)
+            for i in range(per_grp)
+        ]
+    ).astype(jnp.float32)
+    inside = (at >= 0) & (at < quarter)
+    picked = jnp.where(inside[:, None], picked, 0.0)
+    placed = lax.dynamic_update_slice(
+        jnp.zeros((groups * per_grp, width), jnp.float32), picked, (dp * per_grp, tx * half)
+    )
+    last_rows = lax.psum(placed, ("dp", "tx", "ty"))
     final_rows = normalize(last_rows, final_gain).astype(jnp.bfloat16)
-    vocab_block = arrange(lax.all_gather(w_vocab.astype(jnp.bfloat16), "dp", axis=0, tiled=True))
-    logits = jnp.dot(final_rows, vocab_block, preferred_element_type=jnp.float32)
+    mine = lax.dynamic_slice_in_dim(final_rows, block_owner[dp] * rows, rows, 1)
+    partial = dot32(mine, w_vocab.astype(jnp.bfloat16))
+    logits = lax.psum_scatter(partial, "dp", scatter_dimension=0, tiled=True)
     return (layer_out, logits)
 
 

time: 1010 us -> 465 us (0.46)
  waiting for transfers between devices: 685 us -> 305 us
  local copies, waits for them, and re-layouts: 119 us -> 33.8 us
  other arithmetic: 68.5 us -> 10.3 us
  matrix products: 69.7 us -> 12.6 us
  Pallas kernels: 0 us -> 28.5 us
    all_gather x7 -> x6, waiting for transfers between devices: 640 us -> 154 us  [the longest x1 58.6 us: split_heads(): x_all = lax.all_gather(inputs, 'ty', axis=1, tiled=True)]
    psum x0 -> x1, waiting for transfers between devices: none -> 116 us  [shards(): last_rows = lax.psum(placed, ('dp', 'tx', 'ty'))]
    gather x11 -> x1, local copies, waits for them, and re-layouts: 61.2 us -> 1.84 us  [split_heads(): wo = jnp.take(wo, inverse, axis=0).reshape(tx_size, half, piece)]
    reduce_scatter x1 -> x0, waiting for transfers between devices: 45 us -> none  [shards(): lax.psum_scatter(partial_value, 'tx', scatter_dimension=2, tiled=True)]
    dot_general x8 -> x2, matrix products: 52.4 us -> 12.6 us  [the longest x1 7.13 us: dot32(): return jnp.dot(left, right, preferred_element_type=jnp.float32)]
    unnamed x8 -> x9, waiting for transfers between devices: 0.13 us -> 35.5 us
    all_to_all x0 -> x2, blocking collectives: none -> 34.6 us  [the longest x1 17.6 us: split_heads(): lax.all_to_all(spread, 'ty', split_axis=0, concat_axis=0, tiled=True)]
    pallas_call x0 -> x1, Pallas kernels: none -> 28.5 us  [attend(): pl.pallas_call(functools.partial(layer_kernel, groups, heads), grid=(per_...]
  transfers between devices with their start and end apart: 8 -> 8, of which waited for: 7 -> 7; matrix products, arithmetic and copies ran while one was open for 11% -> 7% of each run, Pallas kernels for 0% -> 6%
where the time goes in v1:
time: 465 us; the launch traced here: 464 us
  waiting for transfers between devices  305 us (66%)
  blocking collectives  56.1 us (12%)
  local copies, waits for them, and re-layouts  33.8 us (7%)
  Pallas kernels  28.5 us (6%)
  between operations  17.1 us (4%)
  matrix products  12.6 us (3%)
  other arithmetic  10.3 us (2%)
    psum x1, waiting for transfers between devices, shards(): last_rows = lax.psum(placed, ('dp', 'tx', 'ty'))  116 us
    all_gather x1, waiting for transfers between devices, split_heads(): x_all = lax.all_gather(inputs, 'ty', axis=1, tiled=True)  58.6 us
    unnamed x9, waiting for transfers between devices  35.5 us
    all_gather x1, waiting for transfers between devices, split_heads(): wq = lax.all_gather(wq, 'dp', axis=0, tiled=True)  32.8 us
    pallas_call x1, Pallas kernels, attend(): pl.pallas_call(functools.partial(layer_kernel, groups, heads), grid=(per_...  28.5 us
    all_gather x1, waiting for transfers between devices, split_heads(): wo = lax.all_gather(wo, 'dp', axis=0, tiled=False)  25.9 us
    all_gather x1, blocking collectives, split_heads(): wb = lax.all_gather(w_up_kv.astype(jnp.bfloat16), 'dp', axis=0, tiled=True)  21.6 us
    all_gather x1, waiting for transfers between devices, split_heads(): wa = lax.all_gather(wa, 'dp', axis=0, tiled=True)  19.6 us
  transfers between devices with their start and end apart: 8, of which 7 were waited for; matrix products, arithmetic and copies ran while one was open for 7% of the time, Pallas kernels for 6%

profile of v1, /device:TPU:0, one launch (start us, length us, event | category | flops | bytes accessed | tf_op | source)
XLA Modules:
  0.0 464.0 jit_solution(4771751482931364784)
XLA Ops:
  7.2 0.0 copy-start
  7.2 0.0 all-gather.18.cloned.1.call-start
  7.2 1.5 copy-done
  8.8 0.8 dynamic-slice_convert_fusion
  9.5 0.0 all-gather.18.cloned.1.call-update
  9.5 0.0 all-gather.14.cloned.1.call-start
  9.6 1.3 convert_element_type.29
  10.9 1.1 copy.39
  12.0 0.0 all-gather.14.cloned.1.call-update
  12.0 0.0 all-gather.12.cloned.1.call-start
  12.1 0.2 copy.36
  12.3 0.1 copy.43
  12.5 0.1 copy.38
  12.6 0.8 pad_maximum_fusion.3
  13.4 0.0 all-gather.12.cloned.1.call-update
  13.4 0.0 all-gather.10.cloned.1.call-start
  13.5 0.5 all-gather.10.cloned.1.call-update
  14.0 0.0 all-gather.20.cloned.1.call-start
  14.1 0.1 select_reduce_fusion.inv_ref
  14.2 0.1 reduce_sum.23
  14.3 0.1 broadcast_bitcast_fusion
  14.4 25.9 %all-gather.18.cloned.1.call-done = bf16[2048,256]{1,0:T(8,128)(2,1)} async-done(((bf16[512,256]{1,0:T(8,128)(2,1)}), bf16[2048,256]{1,0:T(8,128)(2,1)}) %all-gather.18.cloned.1.call-update) | async-done | bytes 1048592 | tf_op jit(solution)/shard_map/all_gather | solution.py:271
  40.3 1.8 gather_fusion
  42.2 0.4 bitcast_select_fusion
  42.7 17.0 %all_to_all.10 = bf16[2,1024,256]{2,1,0:T(8,128)(2,1)} all-to-all(bf16[2,1024,256]{2,1,0:T(8,128)(2,1)S(1)} %bitcast_select_fusion), channel_id=1, replica_groups=mesh['dp'=4,'tx'=2,'ty'=4] {'tx'}, dimensions={0} | all-to-all | bytes 2097152 | tf_op jit(solution)/shard_map/all_to_all | solution.py:273
  59.6 0.0 all-gather.20.cloned.1.call-update
  59.6 0.0 all-gather.16.cloned.1.call-start
  59.8 0.6 gather_fusion.1
  60.4 0.6 gather_fusion.2
  61.1 2.0 fusion.4
  63.1 0.9 pad_maximum_fusion.1
  63.9 21.6 %all_gather.33.wb_ref = bf16[512,512]{1,0:T(8,128)(2,1)S(1)} all-gather(bf16[128,512]{1,0:T(8,128)(2,1)S(1)} %convert_element_type.30), channel_id=1, replica_groups=mesh['dp'=4,'tx'=2,'ty'=4] {'dp'}, dimensions={0}, use_global_device_ids=true | all-gather | bytes 655360 | tf_op jit(solution)/shard_map/all_gather | solution.py:255
  85.5 19.6 %all-gather.14.cloned.1.call-done = bf16[2048,576]{1,0:T(8,128)(2,1)} async-done(((bf16[512,576]{1,0:T(8,128)(2,1)}), bf16[2048,576]{1,0:T(8,128)(2,1)}) %all-gather.14.cloned.1.call-update) | async-done | bytes 2359312 | tf_op jit(solution)/shard_map/all_gather | solution.py:252
  105.1 1.1 slice.28
  106.2 3.6 pad_maximum_fusion.wa_ref
  109.8 32.8 %all-gather.12.cloned.1.call-done.wq_ref = bf16[2048,384]{1,0:T(8,128)(2,1)} async-done(((bf16[512,384]{1,0:T(8,128)(2,1)}), bf16[2048,384]{1,0:T(8,128)(2,1)}) %all-gather.12.cloned.1.call-update) | async-done | bytes 1572880 | tf_op jit(solution)/shard_map/all_gather | solution.py:254
  142.6 58.6 %all-gather.10.cloned.1.call-done.x_ref = bf16[2,1024,2048]{2,1,0:T(8,128)(2,1)} async-done(((bf16[2,256,2048]{2,1,0:T(8,128)(2,1)}), bf16[2,1024,2048]{2,1,0:T(8,128)(2,1)}) %all-gather.10.cloned.1.call-update) | async-done | bytes 8388624 | tf_op jit(solution)/shard_map/all_gather | solution.py:251
  201.2 1.4 copy-done.2
  202.6 28.5 %shard_map.131 = bf16[2,1024,256]{2,1,0:T(8,128)(2,1)S(1)} custom-call(s32[4]{0:T(128)S(1)} %select_reduce_fusion.inv_ref, s32[2]{0:T(128)S(1)} %get-tuple-element.5.live_ref, bf16[2,1024,2048]{2,1,0:T(8,128)(2,1)} %all-gather.10.cloned.1.call-done.x_ref, f32[1,2048]{1,0:T(1,128)S(1)} %bitcast.37, f32[1,512]{1,0:T(1,128)S(1)} %bitcast.38, ...), custom_call_target="tpu_custom_call" | custom-call | flops 20000000000 | bytes 16000000 | tf_op jit(solution)/shard_map/pallas_call | solution.py:109
  231.1 0.1 copy.46
  231.2 17.6 %all_to_all.11 = bf16[4,2,256,256]{3,2,1,0:T(8,128)(2,1)} all-to-all(bf16[4,2,256,256]{3,2,1,0:T(8,128)(2,1)S(1)} %bitcast.41), channel_id=1, replica_groups=mesh['dp'=4,'tx'=2,'ty'=4] {'ty'}, dimensions={0} | all-to-all | bytes 2097152 | tf_op jit(solution)/shard_map/all_to_all | solution.py:278
  248.8 0.0 all-gather.16.cloned.1.call-update
  248.9 0.2 all-reduce.4.cloned.1.call-start
  249.1 0.6 fusion.12
  251.0 0.0 all-gather.20.cloned.1.call-done
  251.0 6.6 %copy.42 = bf16[1024,8,256]{2,1,0:T(8,128)(2,1)} copy(bf16[1024,8,256]{2,0,1:T(8,128)(2,1)} %bitcast.40) | data formatting | bytes 8388608 | tf_op jit(solution)/shard_map/transpose | solution.py:284
  257.6 7.5 %reshape.127 = bf16[1024,2048,1]{1,0,2:T(8,128)(2,1)} reshape(bf16[1024,8,256]{2,1,0:T(8,128)(2,1)} %copy.42) | data formatting | bytes 8388608 | tf_op jit(solution)/shard_map/reshape | solution.py:284
  265.0 17.1 %all-gather.16.cloned.1.call-done = bf16[8,2,256,256]{3,2,1,0:T(8,128)(2,1)} async-done(((bf16[4,2,256,256]{3,2,1,0:T(8,128)(2,1)}), bf16[8,2,256,256]{3,2,1,0:T(8,128)(2,1)}) %all-gather.16.cloned.1.call-update) | async-done | bytes 2097168 | tf_op jit(solution)/shard_map/all_gather | solution.py:279
  282.1 2.8 copy.41
  284.9 2.4 dot_general.8
  287.3 5.5 %add_convert_fusion = bf16[2,256,1024]{2,1,0:T(8,128)(2,1)S(1)} fusion(bf16[2,256,2048]{2,1,0:T(8,128)(2,1)} %dot_general.8, bf16[1024,2048,1]{1,0,2:T(8,128)(2,1)} %reshape.127, bf16[2,256,2048]{2,1,0:T(8,128)(2,1)} %param.14, s32[]{:T(128)S(6)} %select_n.55), kind=kOutput, calls=%fused_computation.6 | convolution fusion | flops 2149056512 | bytes 8388612 | tf_op jit(solution)/shard_map/dot_general | solution.py:280
  292.8 0.1 select_dynamic-update-slice_fusion
  292.9 0.8 copy-done.9
  293.7 0.0 all-reduce.4.cloned.1.call-update
  293.7 0.0 all-reduce.6.cloned.1.call-start
  293.7 0.6 dynamic_slice.22
  295.0 0.8 dynamic-slice.2
  295.8 115.6 %all-reduce.4.cloned.1.call-done = f32[8,2048]{1,0:T(8,128)} async-done(((f32[8,2048]{1,0:T(8,128)}), f32[8,2048]{1,0:T(8,128)}) %all-reduce.4.cloned.1.call-update) | async-done | bytes 65552 | tf_op jit(solution)/shard_map/psum | solution.py:338
  411.4 1.0 multiply_reduce_fusion
  412.4 7.1 %fusion = f32[8,7168]{1,0:T(8,128)} fusion(f32[512,7168]{1,0:T(8,128)} %param.25, f32[8,2048]{1,0:T(8,128)} %all-reduce.4.cloned.1.call-done, s32[]{:T(128)S(6)} %select_n.64, f32[512]{0:T(512)S(1)} %dynamic-slice.2, f32[8]{0:T(128)S(1)} %add_rsqrt_fusion), kind=kOutput, calls=%fused_computation.3 | convolution fusion | flops 62402560 | bytes 14927908 | tf_op jit(solution)/shard_map/dot_general | solution.py:24
  419.5 0.0 all-reduce.6.cloned.1.call-update
  419.6 0.6 dynamic-slice
  420.8 34.8 %all-reduce.6.cloned.1.call-done = f32[8,7168]{1,0:T(8,128)} async-done(((f32[8,7168]{1,0:T(8,128)}), f32[8,7168]{1,0:T(8,128)}) %all-reduce.6.cloned.1.call-update) | async-done | bytes 229392
  455.6 1.6 constant_dynamic-slice_fusion
  (38 shorter events, 0.2 us)
Async XLA Ops:
  7.2 1.6 copy-start
  7.2 4.9 %copy-start.7 = (f32[512,384]{1,0:T(8,128)S(1)}, f32[512,384]{1,0:T(8,128)}, u32[]{:S(2)}) copy-start(f32[512,384]{1,0:T(8,128)} %param.21) | copy-start | bytes 2359300
  7.2 33.1 %all-gather.18.cloned.1.call-start = ((), (), s32[]{:S(2)}) async-start(), calls=%async_computation.7 | async-start | bytes 1310720 | tf_op jit(solution)/shard_map/all_gather | solution.py:271
  9.5 95.6 %all-gather.14.cloned.1.call-start = ((), (), s32[]{:S(2)}) async-start(), calls=%async_computation.4 | async-start | bytes 3276800 | tf_op jit(solution)/shard_map/all_gather | solution.py:252
  12.0 130.5 %all-gather.12.cloned.1.call-start = ((), (), s32[]{:S(2)}) async-start(), calls=%async_computation.3 | async-start | bytes 1966080 | tf_op jit(solution)/shard_map/all_gather | solution.py:254
  12.3 1.8 copy-start.11
  13.4 187.7 %all-gather.10.cloned.1.call-start = ((), (), s32[]{:S(2)}) async-start(), calls=%async_computation.2 | async-start | bytes 10485760 | tf_op jit(solution)/shard_map/all_gather | solution.py:251
  14.0 237.0 %all-gather.20.cloned.1.call-start = ((), (), s32[]{:S(2)}) async-start(), calls=%async_computation.8 | async-start | bytes 5242880 | tf_op jit(solution)/shard_map/all_gather | solution.py:274
  42.2 17.5 %copy-start.8 = (f32[128,512]{1,0:T(8,128)S(1)}, f32[128,512]{1,0:T(8,128)}, u32[]{:S(2)}) copy-start(f32[128,512]{1,0:T(8,128)} %param.23) | copy-start | bytes 786436
  42.2 17.6 %copy-start.5 = (s32[8]{0:T(128)S(1)}, s32[8]{0:T(128)}, u32[]{:S(2)}) copy-start(s32[8]{0:T(128)} %param.16) | copy-start | bytes 100
  42.2 18.2 %copy-start.6 = (s32[8]{0:T(128)S(1)}, s32[8]{0:T(128)}, u32[]{:S(2)}) copy-start(s32[8]{0:T(128)} %param.15) | copy-start | bytes 100
  59.6 222.5 %all-gather.16.cloned.1.call-start = ((), (), s32[]{:S(2)}) async-start(), calls=%async_computation.6 | async-start | bytes 3145728 | tf_op jit(solution)/shard_map/all_gather | solution.py:279
  106.2 95.0 %copy-start.3 = (f32[2048]{0:T(1024)S(1)}, f32[2048]{0:T(1024)}, u32[]{:S(2)}) copy-start(f32[2048]{0:T(1024)} %param.18) | copy-start | bytes 24580
  106.2 95.0 %copy-start.4 = (f32[512]{0:T(512)S(1)}, f32[512]{0:T(512)}, u32[]{:S(2)}) copy-start(f32[512]{0:T(512)} %param.19) | copy-start | bytes 6148
  201.2 1.4 copy-start.2
  248.9 162.5 %all-reduce.4.cloned.1.call-start = ((), (), s32[]{:S(2)}) async-start(), calls=%async_computation.5 | async-start | bytes 131072 | tf_op jit(solution)/shard_map/psum | solution.py:338
  292.7 164.4 %copy-start.10 = (bf16[2,256,1024]{2,1,0:T(8,128)(2,1)}, bf16[2,256,1024]{2,1,0:T(8,128)(2,1)S(1)}, u32[]{:S(2)}) copy-start(bf16[2,256,1024]{2,1,0:T(8,128)(2,1)S(1)} %add_convert_fusion) | copy-start | bytes 3145732
  292.9 0.8 copy-start.9
  293.7 161.9 %all-reduce.6.cloned.1.call-start = ((), (), s32[]{:S(2)}) async-start(), calls=%async_computation.9 | async-start | bytes 458752
  412.4 7.2 %copy-start.12 = (u32[32]{0:T(128)S(1)}, u32[32]{0:T(128)}, u32[]{:S(2)}) copy-start(u32[32]{0:T(128)} %constant.85) | copy-start | bytes 388
  412.4 44.8 %copy-start.1 = (f32[512,1024]{1,0:T(8,128)S(1)}, f32[512,1024]{1,0:T(8,128)}, u32[]{:S(2)}) copy-start(f32[512,1024]{1,0:T(8,128)} %param.24) | copy-start | bytes 6291460
Sparse Core Ops, SparseCore 0:
  9.7 30.6 all-gather.17
  42.5 62.5 all-gather.13
  106.7 35.8 all-gather.11
  144.0 57.1 all-gather.9
  202.6 34.4 all-gather.19
  249.0 33.1 all-gather.15
  293.8 117.5 all-reduce.3
  419.7 35.8 all-reduce.5

commit v2 on v1

--- a/solution.py
+++ b/solution.py
@@ -22,6 +22,319 @@
 
 def dot32(left, right):
     return jnp.dot(left, right, preferred_element_type=jnp.float32)
+
+
+def remote(src, dst, send, recv, **where):
+    return pltpu.make_async_remote_copy(
+        src_ref=src,
+        dst_ref=dst,
+        send_sem=send,
+        recv_sem=recv,
+        device_id=where,
+        device_id_type=pl.DeviceIdType.MESH,
+    )
+
+
+def greet(**where):
+    pl.semaphore_signal(
+        pltpu.get_barrier_semaphore(),
+        inc=1,
+        device_id=where,
+        device_id_type=pl.DeviceIdType.MESH,
+    )
+
+
+def gather_kernel(
+    groups, chunks, x_ref, wq_ref, wa_ref, wb_ref, wo_ref, xs_ref, wqs_ref, was_ref, wbs_ref,
+    wos_ref, z_send, z_recv, x_send, x_recv, y_send, y_recv, p_send, p_recv, a_send, a_recv,
+    local,
+):
+    dp, tx, ty = lax.axis_index("dp"), lax.axis_index("tx"), lax.axis_index("ty")
+    core = ty % 2
+    partner = ty + 1 - 2 * core
+    across = (ty + 2) % 4
+    other = 1 - tx
+    rows = x_ref.shape[1] // chunks
+    steps = groups - 1
+
+    greet(ty=partner)
+    greet(ty=across)
+    greet(tx=other)
+    barrier = pltpu.get_barrier_semaphore()
+
+    @pl.when(dp > 0)
+    def _():
+        greet(dp=dp - 1)
+
+    @pl.when(dp < groups - 1)
+    def _():
+        greet(dp=dp + 1)
+
+    ends = (dp > 0).astype(jnp.int32) + (dp < groups - 1).astype(jnp.int32)
+    pl.semaphore_wait(barrier, 3 + ends)
+
+    tensors = [
+        (wq_ref, lambda g: wqs_ref.at[g]),
+        (wa_ref, lambda g: was_ref.at[g, core]),
+        (wb_ref, lambda g: wbs_ref.at[g]),
+        (wo_ref, lambda g: wos_ref.at[g]),
+    ]
+
+    def hop(which, way, step):
+        own, slot = tensors[which]
+        sign = 1 - 2 * way
+        block = dp - sign * step
+        runs = (block >= 0) & (block < groups) & (dp + sign >= 0) & (dp + sign < groups)
+        source = own if step == 0 else slot(block)
+        copy = remote(
+            source, slot(block), z_send.at[way, which, step], z_recv.at[way, which, step],
+            dp=dp + sign,
+        )
+        return copy, runs
+
+    def arrival(which, way, step):
+        own, slot = tensors[which]
+        sign = 1 - 2 * way
+        block = dp - sign * (step + 1)
+        copy = remote(
+            own, slot(block), z_send.at[way, which, step], z_recv.at[way, which, step], dp=dp
+        )
+        return copy, (block >= 0) & (block < groups)
+
+    def start_hop(which, step):
+        for way in range(2):
+            copy, runs = hop(which, way, step)
+            pl.when(runs)(copy.start)
+
+    def wait_hop(which, step):
+        for way in range(2):
+            copy, comes = arrival(which, way, step)
+            pl.when(comes)(copy.wait_recv)
+
+    def cut(ref, slot, prompt, k):
+        return ref.at[slot, prompt, pl.ds(k * rows, rows)]
+
+    def crossing(k, slot):
+        src = x_ref.at[tx, pl.ds(k * rows, rows)]
+        return remote(src, cut(xs_ref, slot, tx, k), x_send.at[k], x_recv.at[k], ty=across)
+
+    def sideways(k, prompt):
+        part = cut(xs_ref, across, prompt, k)
+        return remote(part, part, y_send.at[k], y_recv.at[k], tx=other)
+
+    def inward(k, half, slot, prompt):
+        part = cut(xs_ref, slot, prompt, k)
+        return remote(part, part, p_send.at[half, k], p_recv.at[half, k], ty=partner)
+
+    def own_block(slot):
+        return remote(x_ref, xs_ref.at[slot], a_send.at[0], a_recv.at[0], ty=partner)
+
+    def down_half(side):
+        part = was_ref.at[:, side]
+        return remote(part, part, a_send.at[1], a_recv.at[1], ty=partner)
+
+    for k in range(chunks):
+        crossing(k, ty).start()
+        if k < len(tensors):
+            start_hop(k, 0)
+    own_block(ty).start()
+    mine = [pltpu.make_async_copy(x_ref, xs_ref.at[ty], local.at[len(tensors)])]
+    for which, (own, slot) in enumerate(tensors):
+        mine.append(pltpu.make_async_copy(own, slot(dp), local.at[which]))
+    for copy in mine:
+        copy.start()
+
+    for k in range(chunks):
+        crossing(k, across).wait_recv()
+        sideways(k, tx).start()
+        inward(k, 0, across, tx).start()
+        if k < len(tensors):
+            wait_hop(k, 0)
+            if steps > 1:
+                start_hop(k, 1)
+    for k in range(chunks):
+        sideways(k, other).wait_recv()
+        inward(k, 1, across, other).start()
+    for step in range(1, steps):
+        for which in range(len(tensors)):
+            wait_hop(which, step)
+            if step + 1 < steps:
+                start_hop(which, step + 1)
+            if step == steps - 1 and which == 1:
+                mine[2].wait()
+                down_half(core).start()
+
+    mine[0].wait()
+    mine[1].wait()
+    mine[3].wait()
+    mine[4].wait()
+    down_half(1 - core).wait_recv()
+    own_block(partner).wait_recv()
+    far = (partner + 2) % 4
+    for k in range(chunks):
+        inward(k, 0, far, tx).wait_recv()
+        inward(k, 1, far, other).wait_recv()
+    for step in range(steps):
+        for which in range(len(tensors)):
+            for way in range(2):
+                copy, runs = hop(which, way, step)
+                pl.when(runs)(copy.wait_send)
+    for k in range(chunks):
+        crossing(k, ty).wait_send()
+        sideways(k, tx).wait_send()
+        inward(k, 0, across, tx).wait_send()
+        inward(k, 1, across, other).wait_send()
+    own_block(ty).wait_send()
+    down_half(core).wait_send()
+
+
+def gather_all(groups, x, wq, wa, wb, wo):
+    chunks = 4
+    steps = max(groups - 1, 1)
+    shape = lambda *dims: jax.ShapeDtypeStruct(dims, jnp.bfloat16)
+    dma = pltpu.SemaphoreType.DMA
+    return pl.pallas_call(
+        functools.partial(gather_kernel, groups, chunks),
+        in_specs=[pl.BlockSpec(memory_space=pl.ANY)] * 5,
+        out_specs=[pl.BlockSpec(memory_space=pl.ANY)] * 5,
+        out_shape=[
+            shape(4, *x.shape),
+            shape(groups, *wq.shape),
+            shape(groups, 2, *wa.shape),
+            shape(groups, *wb.shape),
+            shape(groups, *wo.shape),
+        ],
+        scratch_shapes=[
+            dma((2, 4, steps)), dma((2, 4, steps)),
+            dma((chunks,)), dma((chunks,)), dma((chunks,)), dma((chunks,)),
+            dma((2, chunks)), dma((2, chunks)), dma((2,)), dma((2,)), dma((5,)),
+        ],
+        compiler_params=pltpu.CompilerParams(collective_id=0, has_side_effects=True),
+        cost_estimate=pl.CostEstimate(flops=0, bytes_accessed=100_000_000, transcendentals=0),
+    )(x, wq, wa, wb, wo)
+
+
+def tail_kernel(
+    groups, tx_size, ty_size, vocab_chunk, owner_ref, picked_ref, gain_ref, vocab_ref, out_ref,
+    seen, full, rows_ref, table, part, incoming, t_send, t_recv, r_send, r_recv, l_send, l_recv,
+    v_sem,
+):
+    dp, tx, ty = lax.axis_index("dp"), lax.axis_index("tx"), lax.axis_index("ty")
+    per_grp, half = picked_ref.shape
+    block = table.shape[0]
+    peers = groups * tx_size
+    place = dp * tx_size + tx
+    count = vocab_ref.shape[1] // vocab_chunk
+
+    loads = []
+    for k in range(count):
+        cols = pl.ds(k * vocab_chunk, vocab_chunk)
+        loads.append(
+            pltpu.make_async_copy(vocab_ref.at[:, cols], table.at[:, cols], v_sem.at[k])
+        )
+        loads[-1].start()
+
+    for k in range(1, ty_size):
+        greet(ty=(ty + k) % ty_size)
+    for k in range(1, peers):
+        peer = (place + k) % peers
+        greet(dp=peer // tx_size, tx=peer % tx_size)
+    pl.semaphore_wait(pltpu.get_barrier_semaphore(), ty_size + peers - 2)
+
+    def along_ty(k, slot):
+        return remote(
+            picked_ref, seen.at[slot], t_send.at[k], t_recv.at[k], ty=(ty + k) % ty_size
+        )
+
+    for k in range(1, ty_size):
+        along_ty(k, ty).start()
+    merged = picked_ref[...]
+    for k in range(1, ty_size):
+        slot = (ty + ty_size - k) % ty_size
+        along_ty(k, slot).wait_recv()
+        merged = merged + seen[slot]
+    full[place] = merged
+
+    def along_peers(k, slot):
+        peer = (place + k) % peers
+        return remote(
+            full.at[place], full.at[slot], r_send.at[k], r_recv.at[k],
+            dp=peer // tx_size, tx=peer % tx_size,
+        )
+
+    for k in range(1, peers):
+        along_peers(k, place).start()
+    for k in range(1, peers):
+        along_peers(k, (place + peers - k) % peers).wait_recv()
+    for g in range(groups):
+        for t in range(tx_size):
+            rows_ref[g * per_grp : (g + 1) * per_grp, t * half : (t + 1) * half] = full[
+                g * tx_size + t
+            ]
+    final = normalize(rows_ref[...], gain_ref[...])
+    owner = owner_ref[dp]
+    mine = jnp.zeros((groups * per_grp, block), jnp.float32)
+    for g in range(groups):
+        mine = jnp.where(owner == g, final[:, g * block : (g + 1) * block], mine)
+    mine = mine.astype(jnp.bfloat16)
+    for k in range(count):
+        loads[k].wait()
+        cols = slice(k * vocab_chunk, (k + 1) * vocab_chunk)
+        logits = dot32(mine, table[:, cols].astype(jnp.bfloat16))
+        for g in range(groups):
+            part[g, :, cols] = logits[g * per_grp : (g + 1) * per_grp]
+
+    def along_dp(k, slot):
+        peer = (dp + k) % groups
+        return remote(part.at[peer], incoming.at[slot], l_send.at[k], l_recv.at[k], dp=peer)
+
+    for k in range(1, groups):
+        along_dp(k, dp).start()
+    total = part[dp]
+    for k in range(1, groups):
+        slot = (dp + groups - k) % groups
+        along_dp(k, slot).wait_recv()
+        total = total + incoming[slot]
+    out_ref[...] = total
+    for k in range(1, ty_size):
+        along_ty(k, ty).wait_send()
+    for k in range(1, peers):
+        along_peers(k, place).wait_send()
+    for k in range(1, groups):
+        along_dp(k, dp).wait_send()
+
+
+def tail(groups, tx_size, ty_size, owner, picked, gain, vocab):
+    per_grp, half = picked.shape
+    block, words = vocab.shape
+    vocab_chunk = 512
+    peers = groups * tx_size
+    dma = pltpu.SemaphoreType.DMA
+    vmem = pl.BlockSpec(memory_space=pltpu.VMEM)
+    return pl.pallas_call(
+        functools.partial(tail_kernel, groups, tx_size, ty_size, vocab_chunk),
+        in_specs=[
+            pl.BlockSpec(memory_space=pltpu.SMEM), vmem, vmem, pl.BlockSpec(memory_space=pl.ANY),
+        ],
+        out_specs=vmem,
+        out_shape=jax.ShapeDtypeStruct((per_grp, words), jnp.float32),
+        scratch_shapes=[
+            pltpu.VMEM((ty_size, per_grp, half), jnp.float32),
+            pltpu.VMEM((peers, per_grp, half), jnp.float32),
+            pltpu.VMEM((groups * per_grp, half * tx_size), jnp.float32),
+            pltpu.VMEM((block, words), jnp.float32),
+            pltpu.VMEM((groups, per_grp, words), jnp.float32),
+            pltpu.VMEM((groups, per_grp, words), jnp.float32),
+            dma((ty_size,)), dma((ty_size,)), dma((peers,)), dma((peers,)),
+            dma((groups,)), dma((groups,)), dma((words // vocab_chunk,)),
+        ],
+        compiler_params=pltpu.CompilerParams(
+            collective_id=1, has_side_effects=True, vmem_limit_bytes=40 * 1024 * 1024
+        ),
+        cost_estimate=pl.CostEstimate(
+            flops=100_000_000, bytes_accessed=16_000_000, transcendentals=0
+        ),
+    )(owner, picked, gain, vocab)
 
 
 def layer_kernel(
@@ -39,7 +352,7 @@
             start = pl.multiple_of(inv_ref[g] * up_rows, up_rows)
             up_ref[g * up_rows : (g + 1) * up_rows, :] = wb_ref[pl.ds(start, up_rows), :]
 
-    h_ref[...] = normalize(x_ref[0], again_ref[...]).astype(jnp.bfloat16)
+    h_ref[...] = normalize(x_ref[0, 0], again_ref[...]).astype(jnp.bfloat16)
 
     def project(w_ref):
         total = None
@@ -102,7 +415,7 @@
 
 
 def attend(groups, inverse, live, x, again, lgain, cosine, sine, wq, wa, wb):
-    per_grp, _, width = x.shape
+    _, per_grp, _, width = x.shape
     heads = wb.shape[1] // (2 * NOPE)
     whole = lambda a: pl.BlockSpec(a.shape, lambda p, t: (0,) * a.ndim)
     smem = pl.BlockSpec(memory_space=pltpu.SMEM)
@@ -112,7 +425,7 @@
         in_specs=[
             smem,
             smem,
-            pl.BlockSpec((1, TILE, width), lambda p, t: (p, t, 0)),
+            pl.BlockSpec((1, 1, TILE, width), lambda p, t: (t, p, 0, 0)),
             whole(again),
             whole(lgain),
             pl.BlockSpec((TILE, 128), lambda p, t: (t, 0)),
@@ -246,13 +559,14 @@
     rope_q = wq[:, :, NOPE:].reshape(rows, heads * ROPE)
     rope_q = jnp.pad(rope_q, ((0, 0), (0, -(heads * ROPE) % 128)))
     wq = jnp.concatenate([wq[:, :, :NOPE].reshape(rows, heads * NOPE), rope_q], axis=1)
-    wa = w_down_kv.astype(jnp.bfloat16)
-
-    x_all = lax.all_gather(inputs, "ty", axis=1, tiled=True)
-    wa = lax.all_gather(wa, "dp", axis=0, tiled=True)
-    wa = jnp.concatenate([wa, wa[:, LATENT:]], axis=1)
-    wq = lax.all_gather(wq, "dp", axis=0, tiled=True)
-    wb = lax.all_gather(w_up_kv.astype(jnp.bfloat16), "dp", axis=0, tiled=True)
+    wa = lax.dynamic_slice_in_dim(w_down_kv, (ty % 2) * (rows // 2), rows // 2, 0)
+    wa = jnp.concatenate([wa, wa[:, LATENT:]], axis=1).astype(jnp.bfloat16)
+    piece = w_out.shape[1] // ty_size
+    wo = lax.dynamic_slice_in_dim(w_out, ty * piece, piece, 1).astype(jnp.bfloat16)
+    x_all, wq, wa, wb, wo = gather_all(
+        groups, inputs, wq, wa, w_up_kv.astype(jnp.bfloat16), wo
+    )
+    wq, wa, wb = (w.reshape(-1, w.shape[-1]) for w in (wq, wa, wb))
 
     position = jnp.arange(LEN, dtype=jnp.float32)
     frequency = 10000.0 ** (-jnp.arange(ROPE // 2, dtype=jnp.float32) / (ROPE // 2))
@@ -266,11 +580,10 @@
         wq, wa, wb,
     )
 
-    piece = w_out.shape[1] // ty_size
-    wo = lax.dynamic_slice_in_dim(w_out, ty * piece, piece, 1).astype(jnp.bfloat16)
-    wo = lax.all_gather(wo, "dp", axis=0, tiled=False)
     wo = jnp.take(wo, inverse, axis=0).reshape(tx_size, half, piece)
-    wo = lax.all_to_all(wo, "tx", split_axis=0, concat_axis=0, tiled=True)
+    passed = lax.ppermute(jnp.where(tx == 0, wo[1], wo[0]), "tx", [(0, 1), (1, 0)])
+    kept = jnp.where(tx == 0, wo[0], wo[1])
+    wo = jnp.where(tx == 0, jnp.stack([kept, passed]), jnp.stack([passed, kept]))
     wo = lax.all_gather(wo, "ty", axis=1, tiled=False)
 
     spread = mixed.reshape(per_grp, ty_size, quarter, heads * NOPE)
@@ -315,8 +628,9 @@
     slots = dp * per_grp + jnp.arange(per_grp, dtype=jnp.int32)
     live_len = jnp.take(lengths, jnp.take(prompt_deal, slots))
 
-    rows = w_query.shape[0]
-    layer = split_positions if w_query.shape[1] % (NOPE + ROPE) else split_heads
+    whole_heads = w_query.shape[1] % (NOPE + ROPE) == 0
+    here = whole_heads and (lax.axis_size("tx"), lax.axis_size("ty"), per_grp) == (2, 4, 2)
+    layer = split_heads if here else split_positions
     layer_out = layer(
         inputs, inverse, live_len, attn_gain, latent_gain, w_query, w_down_kv, w_up_kv, w_out
     )
@@ -332,14 +646,10 @@
     ).astype(jnp.float32)
     inside = (at >= 0) & (at < quarter)
     picked = jnp.where(inside[:, None], picked, 0.0)
-    placed = lax.dynamic_update_slice(
-        jnp.zeros((groups * per_grp, width), jnp.float32), picked, (dp * per_grp, tx * half)
-    )
-    last_rows = lax.psum(placed, ("dp", "tx", "ty"))
-    final_rows = normalize(last_rows, final_gain).astype(jnp.bfloat16)
-    mine = lax.dynamic_slice_in_dim(final_rows, block_owner[dp] * rows, rows, 1)
-    partial = dot32(mine, w_vocab.astype(jnp.bfloat16))
-    logits = lax.psum_scatter(partial, "dp", scatter_dimension=0, tiled=True)
+    logits = tail(
+        groups, lax.axis_size("tx"), lax.axis_size("ty"), block_owner, picked, final_gain[None],
+        w_vocab,
+    )
     return (layer_out, logits)
 
 

time: 465 us -> 294 us (0.63)
  waiting for transfers between devices: 305 us -> 63.4 us
  Pallas kernels: 28.5 us -> 150 us
  blocking collectives: 56.1 us -> 17.7 us
  matrix products: 12.6 us -> 5.21 us
  local copies, waits for them, and re-layouts: 33.8 us -> 28.7 us
    all_gather x4 -> x0, waiting for transfers between devices: 137 us -> none  [the longest x1 58.6 us: split_heads(): x_all = lax.all_gather(inputs, 'ty', axis=1, tiled=True)]
    pallas_call x0 -> x2, Pallas kernels: none -> 122 us  [the longest x1 102 us: gather_all(): pl.pallas_call(functools.partial(gather_kernel, groups, chunks), in_specs...]
    psum x1 -> x0, waiting for transfers between devices: 116 us -> none  [shards(): last_rows = lax.psum(placed, ('dp', 'tx', 'ty'))]
    unnamed x9 -> x2, waiting for transfers between devices: 35.5 us -> 0.03 us
    all_gather x1, waiting for transfers between devices: 0.02 us -> 31.9 us  [split_heads(): wo = lax.all_gather(wo, 'ty', axis=1, tiled=False)]
    all_gather x1 -> x0, blocking collectives: 21.6 us -> none  [split_heads(): wb = lax.all_gather(w_up_kv.astype(jnp.bfloat16), 'dp', axis=0, tiled=True)]
    ppermute x0 -> x1, waiting for transfers between devices: none -> 17.2 us  [split_heads(): lax.ppermute(jnp.where(tx == 0, wo[1], wo[0]), 'tx', [(0, 1), (1, 0)])]
    all_to_all x1 -> x0, blocking collectives: 17 us -> none  [split_heads(): wo = lax.all_to_all(wo, 'tx', split_axis=0, concat_axis=0, tiled=True)]
  transfers between devices with their start and end apart: 8 -> 3, of which waited for: 7 -> 3; matrix products, arithmetic and copies ran while one was open for 7% -> 3% of each run, Pallas kernels for 6% -> 0%
where the time goes in v2:
time: 294 us
  Pallas kernels  150 us (51%)
  waiting for transfers between devices  63.4 us (22%)
  local copies, waits for them, and re-layouts  28.7 us (10%)
  blocking collectives  17.7 us (6%)
  between operations  15.7 us (5%)
  other arithmetic  11.2 us (4%)
  matrix products  5.21 us (2%)
    pallas_call x1, Pallas kernels, gather_all(): pl.pallas_call(functools.partial(gather_kernel, groups, chunks), in_specs...  102 us
    all_gather x1, waiting for transfers between devices, split_heads(): wo = lax.all_gather(wo, 'ty', axis=1, tiled=False)  31.9 us
    pallas_call x1, Pallas kernels, attend(): pl.pallas_call(functools.partial(layer_kernel, groups, heads), grid=(per_...  28.4 us
    pallas_call x1, Pallas kernels, tail(): pl.pallas_call(functools.partial(tail_kernel, groups, tx_size, ty_size, v...  19.5 us
    all_to_all x1, blocking collectives, split_heads(): lax.all_to_all(spread, 'ty', split_axis=0, concat_axis=0, tiled=True)  17.7 us
    ppermute x1, waiting for transfers between devices, split_heads(): lax.ppermute(jnp.where(tx == 0, wo[1], wo[0]), 'tx', [(0, 1), (1, 0)])  17.2 us
    all_gather x1, waiting for transfers between devices, split_heads(): spread = lax.all_gather(spread, 'tx', axis=0, tiled=False)  14.2 us
    reshape x1, local copies, waits for them, and re-layouts, split_heads(): jnp.moveaxis(wo.reshape(tx_size * ty_size, half, piece), 0, 1)  7.51 us
  transfers between devices with their start and end apart: 3, of which 3 were waited for; matrix products, arithmetic and copies ran while one was open for 3% of the time, Pallas kernels for 0%

profile of v2, /device:TPU:0, one launch (start us, length us, event | category | flops | bytes accessed | tf_op | source)
XLA Modules:
  0.0 293.9 jit_solution(5685746649443460982)
XLA Ops:
  7.2 0.0 copy-start
  7.2 0.0 copy-start.8
  7.2 0.0 copy-start.9
  7.2 0.0 copy-start.12
  7.2 0.0 all-gather.6.cloned.1.call-start
  7.3 0.5 multiply_power_fusion
  7.8 1.3 copy.30
  9.2 0.8 select_reduce_fusion.inv_ref
  10.0 0.0 copy-done.8
  10.0 0.6 gather_fusion.1
  10.7 0.0 copy-done.9
  10.7 0.6 gather_fusion.2
  11.3 0.0 copy-done.12
  11.3 0.7 convert_element_type.21.wb_ref
  12.0 1.1 constant_dynamic-slice_fusion
  13.1 0.2 copy.38
  13.3 0.8 pad_maximum_fusion.3.wa_ref
  14.2 0.1 copy.37
  14.3 0.1 copy.32
  14.4 3.4 %fusion.2 = (f32[1024,32]{1,0:T(8,128)S(1)}, f32[1024,32]{1,0:T(8,128)S(1)}, f32[1024,32]{1,0:T(8,128)}) fusion(f32[32]{0:T(128)} %multiply_power_fusion), kind=kLoop, calls=%fused_computation.18 | loop fusion | flops 65536 | bytes 393344 | tf_op jit(solution)/shard_map/neg | solution.py:576
  17.8 0.0 copy-done
  17.8 0.7 dynamic-slice_convert_fusion.wo_ref
  18.5 0.8 pad_maximum_fusion.2.wq_ref
  19.3 2.7 pad_maximum_fusion
  22.0 0.0 copy-start.6
  22.1 0.0 copy-start.7
  22.1 102.3 %shard_map.131 = (bf16[4,2,256,2048]{3,2,1,0:T(8,128)(2,1)}, bf16[4,512,384]{2,1,0:T(8,128)(2,1)}, bf16[4,2,256,640]{3,2,1,0:T(8,128)(2,1)}, bf16[4,128,512]{2,1,0:T(8,128)(2,1)}, bf16[4,512,256]{2,1,0:T(8,128)(2,1)}) custom-call(bf16[2,256,2048]{2,1,0:T(8,128)(2,1)} %x_ref.1, bf16[512,384]{1,0:T(8,128)(2,1)} %pad_maximum_fusion.2.wq_ref, ...), custom_call_target="tpu_custom_call" | custom-call | bytes 100000000 | tf_op jit(solution)/shard_map/pallas_call | solution.py:196
  124.4 0.0 copy-done.6
  124.4 0.0 copy-done.7
  124.4 0.0 copy-start.4
  124.4 1.4 copy-done.4
  125.8 0.0 copy-start.5
  125.8 1.0 copy-done.5
  126.9 28.4 %shard_map.132 = bf16[2,1024,256]{2,1,0:T(8,128)(2,1)S(1)} custom-call(s32[4]{0:T(128)S(1)} %select_reduce_fusion.inv_ref, s32[2]{0:T(128)S(1)} %get-tuple-element.15.live_ref, bf16[4,2,256,2048]{3,2,1,0:T(8,128)(2,1)} %get-tuple-element.8.x_ref, f32[1,2048]{1,0:T(1,128)S(1)} %bitcast.39, f32[1,512]{1,0:T(1,128)S(1)} %bitcast.40, ...), custom_call_target="tpu_custom_call" | custom-call | flops 20000000000 | bytes 16000000 | tf_op jit(solution)/shard_map/pallas_call | solution.py:422
  155.3 0.1 copy.42
  155.4 0.0 copy-start.11
  155.4 17.7 %all_to_all.5 = bf16[4,2,256,256]{3,2,1,0:T(8,128)(2,1)} all-to-all(bf16[4,2,256,256]{3,2,1,0:T(8,128)(2,1)S(1)} %bitcast.43), channel_id=1, replica_groups=mesh['dp'=4,'tx'=2,'ty'=4] {'ty'}, dimensions={0} | all-to-all | bytes 2097152 | tf_op jit(solution)/shard_map/all_to_all | solution.py:591
  173.1 0.0 all-gather.6.cloned.1.call-update
  173.2 0.2 all-gather.4.cloned.1.call-start
  173.4 0.0 copy-done.11
  173.4 0.6 gather_fusion
  174.1 0.2 broadcast_select_fusion
  174.2 0.1 broadcast_select_fusion.2
  174.3 1.6 collective-permute-start
  175.9 17.2 %collective-permute-done = bf16[1024,256]{1,0:T(8,128)(2,1)S(1)} collective-permute-done((bf16[1024,256]{1,0:T(8,128)(2,1)S(1)}, bf16[1024,256]{1,0:T(8,128)(2,1)S(1)}, u32[]{:S(2)}, u32[]{:S(2)}) %collective-permute-start) | collective-permute-done | bytes 524320 | tf_op jit(solution)/shard_map/ppermute | solution.py:584
  193.1 1.1 maximum_select_fusion
  194.3 0.0 all-gather.4.cloned.1.call-update
  194.3 0.6 fusion.4
  196.2 14.2 %all-gather.6.cloned.1.call-done = bf16[8,2,256,256]{3,2,1,0:T(8,128)(2,1)} async-done(((bf16[4,2,256,256]{3,2,1,0:T(8,128)(2,1)}), bf16[8,2,256,256]{3,2,1,0:T(8,128)(2,1)}) %all-gather.6.cloned.1.call-update) | async-done | bytes 2097168 | tf_op jit(solution)/shard_map/all_gather | solution.py:592
  210.4 2.8 copy.35
  213.2 2.4 dot_general.5
  215.6 31.9 %all-gather.4.cloned.1.call-done = bf16[2,4,1024,256]{3,2,1,0:T(8,128)(2,1)} async-done(((bf16[2,1,1024,256]{3,2,1,0:T(8,128)(2,1)}), bf16[2,4,1024,256]{3,2,1,0:T(8,128)(2,1)}) %all-gather.4.cloned.1.call-update) | async-done | bytes 4194320 | tf_op jit(solution)/shard_map/all_gather | solution.py:587
  247.5 6.6 %copy.41 = bf16[8,1024,256]{2,0,1:T(8,128)(2,1)} copy(bf16[8,1024,256]{2,1,0:T(8,128)(2,1)} %bitcast.42) | data formatting | bytes 8388608 | tf_op jit(solution)/shard_map/reshape | solution.py:597
  254.1 7.5 %reshape.209 = bf16[1024,2048,1]{1,0,2:T(8,128)(2,1)} reshape(bf16[1024,8,256]{2,1,0:T(8,128)(2,1)} %bitcast.41) | data formatting | bytes 8388608 | tf_op jit(solution)/shard_map/reshape | solution.py:597
  261.6 0.0 copy-done.10
  261.6 5.2 %add_convert_fusion = bf16[2,256,1024]{2,1,0:T(8,128)(2,1)S(1)} fusion(bf16[2,256,2048]{2,1,0:T(8,128)(2,1)} %dot_general.5, bf16[1024,2048,1]{1,0,2:T(8,128)(2,1)} %reshape.209, bf16[2,256,2048]{2,1,0:T(8,128)(2,1)S(1)} %copy-done.10, s32[]{:T(128)S(6)} %select_n.100), kind=kOutput, calls=%fused_computation.4 | convolution fusion | flops 2149056512 | bytes 8388612 | tf_op jit(solution)/shard_map/dot_general | solution.py:593
  266.8 0.0 copy-start.13
  266.8 0.1 convert_select_fusion.picked_ref
  266.9 0.0 copy-done.2
  266.9 0.0 copy-done.3
  266.9 19.5 %shard_map.133 = f32[2,7168]{1,0:T(2,128)S(1)} custom-call(s32[4]{0:T(128)S(1)} %copy-done.3, f32[2,1024]{1,0:T(2,128)S(1)} %convert_select_fusion.picked_ref, f32[1,2048]{1,0:T(1,128)S(1)} %bitcast.36, f32[512,7168]{1,0:T(8,128)} %vocab_ref.1), custom_call_target="tpu_custom_call" | custom-call | flops 100000000 | bytes 16000000 | tf_op jit(solution)/shard_map/pallas_call | solution.py:314
  286.4 0.0 copy-done.13
  286.4 0.6 copy.44
  287.1 0.0 copy-done.1
  (16 shorter events, 0.1 us)
Async XLA Ops:
  7.2 10.6 %copy-start = (f32[512,1024]{1,0:T(8,128)S(1)}, f32[512,1024]{1,0:T(8,128)}, u32[]{:S(2)}) copy-start(f32[512,1024]{1,0:T(8,128)} %param.24) | copy-start | bytes 6291460
  7.2 2.8 copy-start.8
  7.2 3.5 %copy-start.9 = (s32[8]{0:T(128)S(1)}, s32[8]{0:T(128)}, u32[]{:S(2)}) copy-start(s32[8]{0:T(128)} %param.15) | copy-start | bytes 100
  7.2 4.1 %copy-start.12 = (f32[128,512]{1,0:T(8,128)S(1)}, f32[128,512]{1,0:T(8,128)}, u32[]{:S(2)}) copy-start(f32[128,512]{1,0:T(8,128)} %param.23) | copy-start | bytes 786436
  7.2 203.2 %all-gather.6.cloned.1.call-start = ((), (), s32[]{:S(2)}) async-start(), calls=%async_computation.2 | async-start | bytes 3145728 | tf_op jit(solution)/shard_map/all_gather | solution.py:592
  22.0 102.3 %copy-start.6 = (f32[2048]{0:T(1024)S(1)}, f32[2048]{0:T(1024)}, u32[]{:S(2)}) copy-start(f32[2048]{0:T(1024)} %param.18) | copy-start | bytes 24580
  22.1 102.3 %copy-start.7 = (f32[512]{0:T(512)S(1)}, f32[512]{0:T(512)}, u32[]{:S(2)}) copy-start(f32[512]{0:T(512)} %param.19) | copy-start | bytes 6148
  124.4 1.4 copy-start.4
  125.8 1.0 copy-start.5
  155.4 18.0 %copy-start.11 = (bf16[4,512,256]{2,1,0:T(8,128)(2,1)S(1)}, bf16[4,512,256]{2,1,0:T(8,128)(2,1)}, u32[]{:S(2)}) copy-start(bf16[4,512,256]{2,1,0:T(8,128)(2,1)} %get-tuple-element.12) | copy-start | bytes 3145732
  173.2 74.3 %all-gather.4.cloned.1.call-start = ((), (), s32[]{:S(2)}) async-start(), calls=%async_computation.1 | async-start | bytes 5242880 | tf_op jit(solution)/shard_map/all_gather | solution.py:587
  174.3 18.8 %collective-permute-start = (bf16[1024,256]{1,0:T(8,128)(2,1)S(1)}, bf16[1024,256]{1,0:T(8,128)(2,1)S(1)}, u32[]{:S(2)}, u32[]{:S(2)}) collective-permute-start(bf16[1024,256]{1,0:T(8,128)(2,1)S(1)} %bitcast.50), channel_id=1, source_target_pairs={{0,4},{4,0},{1,5},{5,1},{2,6},{6,2},{3,7},{7,3},{8,12},{12,8},{9,1... | collective-permute-start | bytes 1572872 | tf_op jit(solution)/shard_map/ppermute | solution.py:584
  254.1 7.5 %copy-start.10 = (bf16[2,256,2048]{2,1,0:T(8,128)(2,1)S(1)}, bf16[2,256,2048]{2,1,0:T(8,128)(2,1)}, u32[]{:S(2)}) copy-start(bf16[2,256,2048]{2,1,0:T(8,128)(2,1)} %x_ref.1) | copy-start | bytes 6291460
  261.6 5.3 %copy-start.2 = (f32[2048]{0:T(1024)S(1)}, f32[2048]{0:T(1024)}, u32[]{:S(2)}) copy-start(f32[2048]{0:T(1024)} %param.20) | copy-start | bytes 24580
  261.6 5.3 %copy-start.3 = (s32[4]{0:T(128)S(1)}, s32[4]{0:T(128)}, u32[]{:S(2)}) copy-start(s32[4]{0:T(128)} %owner_ref.1) | copy-start | bytes 52
  266.8 19.6 %copy-start.13 = (bf16[2,256,1024]{2,1,0:T(8,128)(2,1)}, bf16[2,256,1024]{2,1,0:T(8,128)(2,1)S(1)}, u32[]{:S(2)}) copy-start(bf16[2,256,1024]{2,1,0:T(8,128)(2,1)S(1)} %add_convert_fusion) | copy-start | bytes 3145732
  266.9 20.2 %copy-start.1 = (f32[512,1024]{1,0:T(8,128)S(1)}, f32[512,1024]{1,0:T(8,128)}, u32[]{:S(2)}) copy-start(f32[512,1024]{1,0:T(8,128)} %param.24) | copy-start | bytes 6291460
Sparse Core Ops, SparseCore 0:
  173.3 37.0 all-gather.5
  212.5 34.9 all-gather.3

commit v3 on v2

--- a/solution.py
+++ b/solution.py
@@ -214,32 +214,27 @@
     )(x, wq, wa, wb, wo)
 
 
-def tail_kernel(
-    groups, tx_size, ty_size, vocab_chunk, owner_ref, picked_ref, gain_ref, vocab_ref, out_ref,
-    seen, full, rows_ref, table, part, incoming, t_send, t_recv, r_send, r_recv, l_send, l_recv,
-    v_sem,
+def load_vocab(vocab_chunk, vocab_ref, table, v_sem):
+    loads = []
+    for k in range(vocab_ref.shape[1] // vocab_chunk):
+        cols = pl.ds(k * vocab_chunk, vocab_chunk)
+        loads.append(
+            pltpu.make_async_copy(vocab_ref.at[:, cols], table.at[:, cols], v_sem.at[k])
+        )
+        loads[-1].start()
+    return loads
+
+
+def next_token(
+    groups, tx_size, ty_size, vocab_chunk, loads, owner_ref, picked_ref, gain_ref, out_ref, seen, full,
+    rows_ref, table, part, incoming, t_send, t_recv, r_send, r_recv, l_send, l_recv,
 ):
     dp, tx, ty = lax.axis_index("dp"), lax.axis_index("tx"), lax.axis_index("ty")
     per_grp, half = picked_ref.shape
     block = table.shape[0]
     peers = groups * tx_size
     place = dp * tx_size + tx
-    count = vocab_ref.shape[1] // vocab_chunk
-
-    loads = []
-    for k in range(count):
-        cols = pl.ds(k * vocab_chunk, vocab_chunk)
-        loads.append(
-            pltpu.make_async_copy(vocab_ref.at[:, cols], table.at[:, cols], v_sem.at[k])
-        )
-        loads[-1].start()
-
-    for k in range(1, ty_size):
-        greet(ty=(ty + k) % ty_size)
-    for k in range(1, peers):
-        peer = (place + k) % peers
-        greet(dp=peer // tx_size, tx=peer % tx_size)
-    pl.semaphore_wait(pltpu.get_barrier_semaphore(), ty_size + peers - 2)
+    count = len(loads)
 
     def along_ty(k, slot):
         return remote(
@@ -304,6 +299,131 @@
         along_dp(k, dp).wait_send()
 
 
+def tail_kernel(
+    groups, tx_size, ty_size, vocab_chunk, owner_ref, picked_ref, gain_ref, vocab_ref, out_ref,
+    seen, full, rows_ref, table, part, incoming, t_send, t_recv, r_send, r_recv, l_send, l_recv,
+    v_sem,
+):
+    dp, tx, ty = lax.axis_index("dp"), lax.axis_index("tx"), lax.axis_index("ty")
+    peers = groups * tx_size
+    place = dp * tx_size + tx
+    loads = load_vocab(vocab_chunk, vocab_ref, table, v_sem)
+    for k in range(1, ty_size):
+        greet(ty=(ty + k) % ty_size)
+    for k in range(1, peers):
+        peer = (place + k) % peers
+        greet(dp=peer // tx_size, tx=peer % tx_size)
+    pl.semaphore_wait(pltpu.get_barrier_semaphore(), ty_size + peers - 2)
+    next_token(
+        groups, tx_size, ty_size, vocab_chunk, loads, owner_ref, picked_ref, gain_ref, out_ref,
+        seen, full, rows_ref, table, part, incoming, t_send, t_recv, r_send, r_recv, l_send,
+        l_recv,
+    )
+
+
+def close_kernel(
+    groups, tx_size, ty_size, vocab_chunk, owner_ref, live_ref, o_ref, wo_ref, residual_ref,
+    gain_ref, vocab_ref, hidden_ref, out_ref,
+    heard, wos, total, picked_ref, o_send, o_recv, w_sem, seen, full, rows_ref, table, part,
+    incoming, t_send, t_recv, r_send, r_recv, l_send, l_recv, v_sem,
+):
+    dp, tx, ty = lax.axis_index("dp"), lax.axis_index("tx"), lax.axis_index("ty")
+    plane = tx_size * ty_size
+    spot = tx * ty_size + ty
+    per_grp, quarter, half = residual_ref.shape
+    heads_width = wos.shape[-1]
+
+    weights = pltpu.make_async_copy(wo_ref, wos, w_sem.at[0])
+    weights.start()
+    for k in range(1, plane):
+        peer = (spot + k) % plane
+        greet(tx=peer // ty_size, ty=peer % ty_size)
+    for k in range(1, groups):
+        for t in range(tx_size):
+            greet(dp=(dp + k) % groups, tx=t)
+    pl.semaphore_wait(pltpu.get_barrier_semaphore(), plane - 1 + (groups - 1) * tx_size)
+
+    def heads_of(k, slot):
+        peer = (spot + k) % plane
+        return remote(
+            o_ref.at[peer % ty_size], heard.at[slot], o_send.at[k], o_recv.at[k],
+            tx=peer // ty_size, ty=peer % ty_size,
+        )
+
+    for k in range(1, plane):
+        heads_of(k, spot).start()
+    loads = load_vocab(vocab_chunk, vocab_ref, table, v_sem)
+    weights.wait()
+    for k in (0,) + tuple(range(1, plane)):
+        source = (spot + plane - k) % plane
+        if k:
+            heads_of(k, source).wait_recv()
+        for p in range(per_grp):
+            block = o_ref[ty, p] if k == 0 else heard[source, p]
+            term = lax.dot_general(
+                block, wos[source], (((1,), (1,)), ((), ())),
+                preferred_element_type=jnp.float32,
+            )
+            total[p] = term if k == 0 else total[p] + term
+    row = lax.broadcasted_iota(jnp.int32, (quarter, half), 0)
+    for p in range(per_grp):
+        hidden = (residual_ref[p].astype(jnp.float32) + total[p]).astype(jnp.bfloat16)
+        hidden_ref[p] = hidden
+        last = row == live_ref[p] - 1 - ty * quarter
+        picked_ref[p : p + 1, :] = jnp.sum(
+            jnp.where(last, hidden.astype(jnp.float32), 0.0), axis=0, keepdims=True
+        )
+    next_token(
+        groups, tx_size, ty_size, vocab_chunk, loads, owner_ref, picked_ref, gain_ref, out_ref,
+        seen, full, rows_ref, table, part, incoming, t_send, t_recv, r_send, r_recv, l_send,
+        l_recv,
+    )
+    for k in range(1, plane):
+        heads_of(k, spot).wait_send()
+
+
+def close(groups, tx_size, ty_size, owner, live, mixed, wo, residual, gain, vocab):
+    per_grp, quarter, half = residual.shape
+    block, words = vocab.shape
+    vocab_chunk = 512
+    peers = groups * tx_size
+    plane = tx_size * ty_size
+    dma = pltpu.SemaphoreType.DMA
+    vmem = pl.BlockSpec(memory_space=pltpu.VMEM)
+    smem = pl.BlockSpec(memory_space=pltpu.SMEM)
+    hbm = pl.BlockSpec(memory_space=pl.ANY)
+    return pl.pallas_call(
+        functools.partial(close_kernel, groups, tx_size, ty_size, vocab_chunk),
+        in_specs=[smem, smem, vmem, hbm, vmem, vmem, hbm],
+        out_specs=[vmem, vmem],
+        out_shape=[
+            jax.ShapeDtypeStruct(residual.shape, jnp.bfloat16),
+            jax.ShapeDtypeStruct((per_grp, words), jnp.float32),
+        ],
+        scratch_shapes=[
+            pltpu.VMEM((plane,) + mixed.shape[1:], jnp.bfloat16),
+            pltpu.VMEM(wo.shape, jnp.bfloat16),
+            pltpu.VMEM(residual.shape, jnp.float32),
+            pltpu.VMEM((per_grp, half), jnp.float32),
+            dma((plane,)), dma((plane,)), dma((1,)),
+            pltpu.VMEM((ty_size, per_grp, half), jnp.float32),
+            pltpu.VMEM((peers, per_grp, half), jnp.float32),
+            pltpu.VMEM((groups * per_grp, half * tx_size), jnp.float32),
+            pltpu.VMEM((block, words), jnp.float32),
+            pltpu.VMEM((groups, per_grp, words), jnp.float32),
+            pltpu.VMEM((groups, per_grp, words), jnp.float32),
+            dma((ty_size,)), dma((ty_size,)), dma((peers,)), dma((peers,)),
+            dma((groups,)), dma((groups,)), dma((words // vocab_chunk,)),
+        ],
+        compiler_params=pltpu.CompilerParams(
+            collective_id=3, has_side_effects=True, vmem_limit_bytes=48 * 1024 * 1024
+        ),
+        cost_estimate=pl.CostEstimate(
+            flops=3_000_000_000, bytes_accessed=24_000_000, transcendentals=0
+        ),
+    )(owner, live, mixed, wo, residual, gain, vocab)
+
+
 def tail(groups, tx_size, ty_size, owner, picked, gain, vocab):
     per_grp, half = picked.shape
     block, words = vocab.shape
@@ -338,29 +458,50 @@
 
 
 def layer_kernel(
-    groups, heads, inv_ref, live_ref, x_ref, again_ref, lgain_ref, cos_ref, sin_ref,
-    wq_ref, wa_ref, wb_ref, o_ref, h_ref, up_ref, k_ref, v_ref,
+    heads, live_ref, x_ref, again_ref, lgain_ref, cos_ref, sin_ref,
+    wq_ref, wa_ref, wb_ref, keep_ref, give_ref, o_ref, wos_ref, h_ref, k_ref, v_ref,
+    send, recv, local,
 ):
     prompt, tile = pl.program_id(0), pl.program_id(1)
+    moment = prompt * (LEN // TILE) + tile
+    tx, ty = lax.axis_index("tx"), lax.axis_index("ty")
+    partner = ty + 1 - 2 * (ty % 2)
+    across = (ty + 2) % 4
+    far = (partner + 2) % 4
+    other = 1 - tx
+
+    def move(n, source, slot_tx, slot_ty, **where):
+        return remote(source, wos_ref.at[slot_tx, slot_ty], send.at[n], recv.at[n], **where)
+
+    def passed(n, slot_tx, slot_ty, **where):
+        return move(n, wos_ref.at[slot_tx, slot_ty], slot_tx, slot_ty, **where)
+
+    @pl.when(moment == 0)
+    def _():
+        greet(tx=other)
+        greet(ty=partner)
+        greet(ty=across)
+        pl.semaphore_wait(pltpu.get_barrier_semaphore(), 3)
+        move(0, give_ref, tx, ty, tx=other).start()
+        move(1, keep_ref, tx, ty, ty=across).start()
+        move(2, keep_ref, tx, ty, ty=partner).start()
+        pltpu.make_async_copy(keep_ref, wos_ref.at[tx, ty], local.at[0]).start()
+
+    @pl.when(moment == 3)
+    def _():
+        move(0, give_ref, other, ty, tx=other).wait_recv()
+        passed(3, other, ty, ty=across).start()
+        passed(4, other, ty, ty=partner).start()
+        move(1, keep_ref, tx, across, ty=across).wait_recv()
+        passed(5, tx, across, ty=partner).start()
+
+    @pl.when(moment == 6)
+    def _():
+        move(3, keep_ref, other, across, ty=across).wait_recv()
+        passed(6, other, across, ty=partner).start()
+
     width = x_ref.shape[-1]
-    rows = width // groups
-    up_rows = LATENT // groups
-
-    @pl.when((prompt == 0) & (tile == 0))
-    def _():
-        for g in range(groups):
-            start = pl.multiple_of(inv_ref[g] * up_rows, up_rows)
-            up_ref[g * up_rows : (g + 1) * up_rows, :] = wb_ref[pl.ds(start, up_rows), :]
-
     h_ref[...] = normalize(x_ref[0, 0], again_ref[...]).astype(jnp.bfloat16)
-
-    def project(w_ref):
-        total = None
-        for g in range(groups):
-            start = pl.multiple_of(inv_ref[g] * rows, rows)
-            part = dot32(h_ref[:, g * rows : (g + 1) * rows], w_ref[pl.ds(start, rows), :])
-            total = part if total is None else total + part
-        return total
 
     cosine, sine = cos_ref[...], sin_ref[...]
     lane = lax.broadcasted_iota(jnp.int32, (TILE, 128), 1)
@@ -373,17 +514,17 @@
         )
         return block * cosine + swapped * sine
 
-    down = project(wa_ref)
+    down = dot32(h_ref[...], wa_ref[...])
     latent = normalize(down[:, :LATENT], lgain_ref[...]).astype(jnp.bfloat16)
     key_rope = rotate(down[:, LATENT:]).astype(jnp.bfloat16)
-    key_val = dot32(latent, up_ref[...]).astype(jnp.bfloat16)
+    key_val = dot32(latent, wb_ref[...]).astype(jnp.bfloat16)
     here = pl.ds(pl.multiple_of(tile * TILE, TILE), TILE)
     for head in range(heads):
         k_ref[head, here, :NOPE] = key_val[:, 2 * head * NOPE : (2 * head + 1) * NOPE]
         k_ref[head, here, NOPE:] = key_rope
         v_ref[head, here, :] = key_val[:, (2 * head + 1) * NOPE : (2 * head + 2) * NOPE]
 
-    queries = project(wq_ref)
+    queries = dot32(h_ref[...], wq_ref[...])
     nope = queries[:, : heads * NOPE].astype(jnp.bfloat16)
     query = []
     for head in range(heads):
@@ -411,19 +552,35 @@
                 expo = jnp.exp(score - jnp.max(score, axis=-1, keepdims=True))
                 prob = expo * (1.0 / jnp.sum(expo, axis=-1, keepdims=True))
                 out = dot32(prob.astype(jnp.bfloat16), v_ref[head, :span, :])
-                o_ref[0, :, head * NOPE : (head + 1) * NOPE] = out.astype(jnp.bfloat16)
-
-
-def attend(groups, inverse, live, x, again, lgain, cosine, sine, wq, wa, wb):
+                o_ref[0, 0, :, head * NOPE : (head + 1) * NOPE] = out.astype(jnp.bfloat16)
+
+    @pl.when(moment == 7)
+    def _():
+        move(2, keep_ref, tx, partner, ty=partner).wait_recv()
+        move(4, keep_ref, other, partner, ty=partner).wait_recv()
+        move(5, keep_ref, tx, far, ty=partner).wait_recv()
+        move(6, keep_ref, other, far, ty=partner).wait_recv()
+        move(0, give_ref, tx, ty, tx=other).wait_send()
+        move(1, keep_ref, tx, ty, ty=across).wait_send()
+        move(2, keep_ref, tx, ty, ty=partner).wait_send()
+        passed(3, other, ty, ty=across).wait_send()
+        passed(4, other, ty, ty=partner).wait_send()
+        passed(5, tx, across, ty=partner).wait_send()
+        passed(6, other, across, ty=partner).wait_send()
+        pltpu.make_async_copy(keep_ref, wos_ref.at[tx, ty], local.at[0]).wait()
+
+
+def attend(
+    live, x, again, lgain, cosine, sine, wq, wa, wb, keep, give
+):
     _, per_grp, _, width = x.shape
     heads = wb.shape[1] // (2 * NOPE)
     whole = lambda a: pl.BlockSpec(a.shape, lambda p, t: (0,) * a.ndim)
     smem = pl.BlockSpec(memory_space=pltpu.SMEM)
     return pl.pallas_call(
-        functools.partial(layer_kernel, groups, heads),
+        functools.partial(layer_kernel, heads),
         grid=(per_grp, LEN // TILE),
         in_specs=[
-            smem,
             smem,
             pl.BlockSpec((1, 1, TILE, width), lambda p, t: (t, p, 0, 0)),
             whole(again),
@@ -433,20 +590,32 @@
             whole(wq),
             whole(wa),
             whole(wb),
-        ],
-        out_specs=pl.BlockSpec((1, TILE, heads * NOPE), lambda p, t: (p, t, 0)),
-        out_shape=jax.ShapeDtypeStruct((per_grp, LEN, heads * NOPE), jnp.bfloat16),
+            pl.BlockSpec(memory_space=pl.ANY),
+            pl.BlockSpec(memory_space=pl.ANY),
+        ],
+        out_specs=[
+            pl.BlockSpec((1, 1, TILE, heads * NOPE), lambda p, t: (t, p, 0, 0)),
+            pl.BlockSpec(memory_space=pl.ANY),
+        ],
+        out_shape=[
+            jax.ShapeDtypeStruct((LEN // TILE, per_grp, TILE, heads * NOPE), jnp.bfloat16),
+            jax.ShapeDtypeStruct((2, 4) + keep.shape, jnp.bfloat16),
+        ],
         scratch_shapes=[
             pltpu.VMEM((TILE, width), jnp.bfloat16),
-            pltpu.VMEM(wb.shape, jnp.bfloat16),
             pltpu.VMEM((heads, LEN, 2 * NOPE), jnp.bfloat16),
             pltpu.VMEM((heads, LEN, NOPE), jnp.bfloat16),
-        ],
-        compiler_params=pltpu.CompilerParams(vmem_limit_bytes=48 * 1024 * 1024),
+            pltpu.SemaphoreType.DMA((7,)),
+            pltpu.SemaphoreType.DMA((7,)),
+            pltpu.SemaphoreType.DMA((1,)),
+        ],
+        compiler_params=pltpu.CompilerParams(
+            collective_id=2, has_side_effects=True, vmem_limit_bytes=48 * 1024 * 1024
+        ),
         cost_estimate=pl.CostEstimate(
             flops=20_000_000_000, bytes_accessed=16_000_000, transcendentals=4_000_000
         ),
-    )(inverse, live, x, again, lgain, cosine, sine, wq, wa, wb)
+    )(live, x, again, lgain, cosine, sine, wq, wa, wb, keep, give)
 
 
 def rotate_half(values, position):
@@ -546,7 +715,8 @@
 
 
 def split_heads(
-    inputs, inverse, live_len, attn_gain, latent_gain, w_query, w_down_kv, w_up_kv, w_out
+    inputs, inverse, live_len, attn_gain, latent_gain, w_query, w_down_kv, w_up_kv, w_out,
+    block_owner, final_gain, w_vocab,
 ):
     groups = lax.axis_size("dp")
     tx_size, ty_size = lax.axis_size("tx"), lax.axis_size("ty")
@@ -566,7 +736,9 @@
     x_all, wq, wa, wb, wo = gather_all(
         groups, inputs, wq, wa, w_up_kv.astype(jnp.bfloat16), wo
     )
-    wq, wa, wb = (w.reshape(-1, w.shape[-1]) for w in (wq, wa, wb))
+    wq, wa, wb = (
+        jnp.take(w, inverse, axis=0).reshape(-1, w.shape[-1]) for w in (wq, wa, wb)
+    )
 
     position = jnp.arange(LEN, dtype=jnp.float32)
     frequency = 10000.0 ** (-jnp.arange(ROPE // 2, dtype=jnp.float32) / (ROPE // 2))
@@ -575,32 +747,23 @@
     cosine = jnp.concatenate([cosine] * 4, axis=1)
     sine = jnp.concatenate([-sine, sine, -sine, sine], axis=1)
 
-    mixed = attend(
-        groups, inverse, live_len, x_all, attn_gain[None], latent_gain[None], cosine, sine,
-        wq, wa, wb,
-    )
-
-    wo = jnp.take(wo, inverse, axis=0).reshape(tx_size, half, piece)
-    passed = lax.ppermute(jnp.where(tx == 0, wo[1], wo[0]), "tx", [(0, 1), (1, 0)])
-    kept = jnp.where(tx == 0, wo[0], wo[1])
-    wo = jnp.where(tx == 0, jnp.stack([kept, passed]), jnp.stack([passed, kept]))
-    wo = lax.all_gather(wo, "ty", axis=1, tiled=False)
-
-    spread = mixed.reshape(per_grp, ty_size, quarter, heads * NOPE)
-    spread = jnp.moveaxis(spread, 1, 0)
-    spread = lax.all_to_all(spread, "ty", split_axis=0, concat_axis=0, tiled=True)
-    spread = lax.all_gather(spread, "tx", axis=0, tiled=False)
-    branch = lax.dot_general(
-        jnp.moveaxis(spread.reshape(tx_size * ty_size, per_grp * quarter, -1), 0, 1).reshape(
-            per_grp * quarter, -1
-        ),
-        jnp.moveaxis(wo.reshape(tx_size * ty_size, half, piece), 0, 1).reshape(half, -1),
-        (((1,), (1,)), ((), ())),
-        preferred_element_type=jnp.float32,
-    ).reshape(per_grp, quarter, half)
+    share = groups // tx_size
+
+    def model_rows(which):
+        blocks = lax.dynamic_slice_in_dim(inverse, which * share, share)
+        return jnp.take(wo, blocks, axis=0).reshape(half, piece)
+
+    mixed, wo = attend(
+        live_len, x_all, attn_gain[None], latent_gain[None], cosine, sine,
+        wq, wa, wb, model_rows(tx), model_rows(1 - tx),
+    )
     residual = lax.dynamic_slice_in_dim(inputs, tx * half, half, 2)
-    layer_out = (residual.astype(jnp.float32) + branch).astype(jnp.bfloat16)
-    return layer_out
+    return tuple(
+        close(
+            groups, tx_size, ty_size, block_owner, live_len, mixed,
+            wo.reshape((tx_size * ty_size,) + wo.shape[2:]), residual, final_gain[None], w_vocab,
+        )
+    )
 
 
 def shards(
@@ -630,10 +793,12 @@
 
     whole_heads = w_query.shape[1] % (NOPE + ROPE) == 0
     here = whole_heads and (lax.axis_size("tx"), lax.axis_size("ty"), per_grp) == (2, 4, 2)
-    layer = split_heads if here else split_positions
-    layer_out = layer(
+    arrays = (
         inputs, inverse, live_len, attn_gain, latent_gain, w_query, w_down_kv, w_up_kv, w_out
     )
+    if here and groups > 2 and groups % 2 == 0:
+        return split_heads(*arrays, block_owner, final_gain, w_vocab)
+    layer_out = split_positions(*arrays)
 
     at = live_len - 1 - ty * quarter
     picked = jnp.stack(

time: 294 us -> 216 us (0.73)
  waiting for transfers between devices: 63.4 us -> 0 us
  Pallas kernels: 150 us -> 182 us
  blocking collectives: 17.7 us -> 0 us
  between operations: 15.7 us -> 0.96 us
  local copies, waits for them, and re-layouts: 28.7 us -> 18.8 us
  matrix products: 5.21 us -> 0 us
    all_gather x2 -> x0, waiting for transfers between devices: 46.1 us -> none  [the longest x1 31.9 us: split_heads(): wo = lax.all_gather(wo, 'ty', axis=1, tiled=False)]
    pallas_call x2, Pallas kernels: 47.9 us -> 80 us  [the longest x1 43.1 us: close(): pl.pallas_call(functools.partial(close_kernel, groups, tx_size, ty_size,...]
    all_to_all x1 -> x0, blocking collectives: 17.7 us -> none  [split_heads(): lax.all_to_all(spread, 'ty', split_axis=0, concat_axis=0, tiled=True)]
    ppermute x1 -> x0, waiting for transfers between devices: 17.2 us -> none  [split_heads(): lax.ppermute(jnp.where(tx == 0, wo[1], wo[0]), 'tx', [(0, 1), (1, 0)])]
    reshape x3 -> x0, local copies, waits for them, and re-layouts: 14.2 us -> none  [the longest x1 7.51 us: split_heads(): jnp.moveaxis(wo.reshape(tx_size * ty_size, half, piece), 0, 1)]
    gather x1 -> x5, local copies, waits for them, and re-layouts: 0.61 us -> 11.6 us  [the longest x3 7.98 us: split_heads(): jnp.take(w, inverse, axis=0).reshape(-1, w.shape[-1])]
    select_n x5, other arithmetic: 1.45 us -> 7.76 us  [the longest x4 6.62 us: split_heads(): jnp.take(w, inverse, axis=0).reshape(-1, w.shape[-1])]
    dot_general x1 -> x0, matrix products: 5.21 us -> none  [split_heads(): lax.dot_general(jnp.moveaxis(spread.reshape(tx_size * ty_size, per_grp *...]
  transfers between devices with their start and end apart: 3 -> 0, of which waited for: 3 -> 0; matrix products, arithmetic and copies ran while one was open for 3% -> 0% of each run, Pallas kernels for 0% -> 0%
where the time goes in v3:
time: 216 us
  Pallas kernels  182 us (84%)
  local copies, waits for them, and re-layouts  18.8 us (9%)
  other arithmetic  14.1 us (7%)
    pallas_call x1, Pallas kernels, gather_all(): pl.pallas_call(functools.partial(gather_kernel, groups, chunks), in_specs...  102 us
    pallas_call x1, Pallas kernels, close(): pl.pallas_call(functools.partial(close_kernel, groups, tx_size, ty_size,...  43.1 us
    pallas_call x1, Pallas kernels, attend(): pl.pallas_call(functools.partial(layer_kernel, heads), grid=(per_grp, LEN...  36.9 us
    gather x3, local copies, waits for them, and re-layouts, split_heads(): jnp.take(w, inverse, axis=0).reshape(-1, w.shape[-1])  7.98 us
    select_n x4, other arithmetic, split_heads(): jnp.take(w, inverse, axis=0).reshape(-1, w.shape[-1])  6.62 us

profile of v3, /device:TPU:0, one launch (start us, length us, event | category | flops | bytes accessed | tf_op | source)
XLA Modules:
  0.0 216.1 jit_solution(2165622067653122231)
XLA Ops:
  0.6 0.0 copy-start
  0.6 0.0 copy-start.11
  0.7 1.2 constant_dynamic-slice_fusion.1
  1.9 0.2 copy.24
  2.1 0.8 pad_maximum_fusion.3.wa_ref
  3.0 0.0 copy-done
  3.0 0.8 dynamic-slice_convert_fusion.wo_ref
  3.7 0.0 copy-done.11
  3.7 0.2 copy.19
  3.9 0.1 copy.23
  4.1 0.1 copy.21
  4.2 0.0 copy-start.6
  4.2 0.8 pad_maximum_fusion.2.wq_ref
  5.0 1.6 convert_element_type.11.wb_ref
  6.6 102.3 %shard_map.131 = (bf16[4,2,256,2048]{3,2,1,0:T(8,128)(2,1)}, bf16[4,512,384]{2,1,0:T(8,128)(2,1)}, bf16[4,2,256,640]{3,2,1,0:T(8,128)(2,1)}, bf16[4,128,512]{2,1,0:T(8,128)(2,1)}, bf16[4,512,256]{2,1,0:T(8,128)(2,1)}) custom-call(bf16[2,256,2048]{2,1,0:T(8,128)(2,1)} %x_ref.1, bf16[512,384]{1,0:T(8,128)(2,1)} %pad_maximum_fusion.2.wq_ref, ...), custom_call_target="tpu_custom_call" | custom-call | bytes 100000000 | tf_op jit(solution)/shard_map/pallas_call | solution.py:196
  108.9 0.0 copy-done.6
  108.9 0.1 select_reduce_fusion
  109.0 0.1 compare_and_fusion
  109.1 1.8 gather_fusion.6
  111.0 1.8 gather_fusion.5
  112.8 1.1 broadcast_select_fusion
  113.9 4.1 %gather_fusion.1 = bf16[4,2,256,640]{3,2,1,0:T(8,128)(2,1)} fusion(bf16[4,2,256,640]{3,2,1,0:T(8,128)(2,1)} %get-tuple-element.13, s32[1024]{0:T(1024)S(1)} %pad_clamp_fusion.2), kind=kCustom, calls=%fused_computation.5 | custom fusion | bytes 5242896 | tf_op jit(solution)/shard_map/jit(_take)/gather | solution.py:740
  118.0 0.1 broadcast_in_dim.88
  118.1 3.1 %bitcast_select_fusion.wa_ref = bf16[2048,640]{1,0:T(8,128)(2,1)} fusion(bf16[4,2,256,640]{3,2,1,0:T(8,128)(2,1)} %gather_fusion.1, pred[2048]{0:T(1024)(128)(4,1)S(1)} %broadcast_in_dim.89), kind=kLoop, calls=%fused_computation.7 | loop fusion | flops 1310720 | bytes 5244928 | tf_op jit(solution)/shard_map/jit(_take)/select_n | solution.py:740
  121.2 3.3 %gather_fusion = bf16[4,512,384]{2,1,0:T(8,128)(2,1)} fusion(bf16[4,512,384]{2,1,0:T(8,128)(2,1)} %get-tuple-element.12, s32[1024]{0:T(1024)S(1)} %pad_clamp_fusion.2), kind=kCustom, calls=%fused_computation.4 | custom fusion | bytes 3145744 | tf_op jit(solution)/shard_map/jit(_take)/gather | solution.py:740
  124.6 0.0 copy-start.12
  124.6 0.1 broadcast_bitcast_fusion
  124.7 0.0 copy-start.9
  124.7 2.5 %bitcast_select_fusion.1.wq_ref = bf16[2048,384]{1,0:T(8,128)(2,1)} fusion(bf16[4,512,384]{2,1,0:T(8,128)(2,1)} %gather_fusion, pred[2048]{0:T(1024)(128)(4,1)S(1)} %bitcast.34), kind=kLoop, calls=%fused_computation.8 | loop fusion | flops 786432 | bytes 3147776 | tf_op jit(solution)/shard_map/jit(_take)/select_n | solution.py:740
  127.2 0.0 copy-start.10
  127.2 0.0 copy-done.12
  127.2 0.6 gather_fusion.2
  127.8 0.1 broadcast_bitcast_fusion.1
  127.9 0.9 bitcast_select_fusion.2.wb_ref
  128.8 0.0 copy-done.9
  128.8 0.6 gather_fusion.3
  129.5 0.0 copy-done.10
  129.5 0.6 gather_fusion.4
  130.2 0.0 copy-start.1
  130.2 0.0 copy-start.2
  130.2 0.0 copy-start.3
  130.2 0.0 copy-start.4
  130.2 0.0 copy-start.7
  130.2 0.0 copy-start.8
  130.2 2.0 fusion.2
  132.2 0.9 pad_maximum_fusion
  133.1 0.0 copy-done.1
  133.1 0.0 copy-done.2
  133.1 0.0 copy-done.3
  133.1 0.0 copy-done.4
  133.1 0.0 copy-done.7
  133.1 0.0 copy-done.8
  133.1 36.9 %shard_map.132 = (bf16[4,2,256,256]{3,2,1,0:T(8,128)(2,1)S(1)}, bf16[2,4,1024,256]{3,2,1,0:T(8,128)(2,1)}) custom-call(s32[2]{0:T(128)S(1)} %and_select_fusion.live_ref, bf16[4,2,256,2048]{3,2,1,0:T(8,128)(2,1)} %get-tuple-element.11.x_ref, f32[1,2048]{1,0:T(1,128)S(1)} %bitcast.27, f32[1,512]{1,0:T(1,128)S(1)} %bitcast.28, ...), custom_call_target="tpu_custom_call" | custom-call | flops 20000000000 | bytes 16000000 | tf_op jit(solution)/shard_map/pallas_call | solution.py:580
  170.1 0.0 copy-start.5
  170.1 1.3 constant_dynamic-slice_fusion.residual_ref
  171.4 0.0 copy-done.5
  171.4 43.1 %shard_map.133 = (bf16[2,256,1024]{2,1,0:T(8,128)(2,1)S(1)}, f32[2,7168]{1,0:T(2,128)S(1)}) custom-call(s32[4]{0:T(128)S(1)} %copy-done.6, s32[2]{0:T(128)S(1)} %and_select_fusion.live_ref, bf16[4,2,256,256]{3,2,1,0:T(8,128)(2,1)S(1)} %get-tuple-element.16.o_ref, bf16[8,1024,256]{2,1,0:T(8,128)(2,1)} %bitcast.29, ...), custom_call_target="tpu_custom_call" | custom-call | flops 3000000000 | bytes 24000000 | tf_op jit(solution)/shard_map/pallas_call | solution.py:395
  214.5 1.0 copy.28
  215.5 0.6 copy.29
  (16 shorter events, 0.2 us)
Async XLA Ops:
  0.6 2.3 %copy-start = (f32[512,1024]{1,0:T(8,128)S(1)}, f32[512,1024]{1,0:T(8,128)}, u32[]{:S(2)}) copy-start(f32[512,1024]{1,0:T(8,128)} %param.26) | copy-start | bytes 6291460
  0.6 3.1 %copy-start.11 = (f32[512,384]{1,0:T(8,128)S(1)}, f32[512,384]{1,0:T(8,128)}, u32[]{:S(2)}) copy-start(f32[512,384]{1,0:T(8,128)} %param.23) | copy-start | bytes 2359300
  4.2 104.7 %copy-start.6 = (s32[4]{0:T(128)S(1)}, s32[4]{0:T(128)}, u32[]{:S(2)}) copy-start(s32[4]{0:T(128)} %owner_ref.1) | copy-start | bytes 52
  124.6 2.6 %copy-start.12 = (bf16[4,128,512]{2,1,0:T(8,128)(2,1)S(1)}, bf16[4,128,512]{2,1,0:T(8,128)(2,1)}, u32[]{:S(2)}) copy-start(bf16[4,128,512]{2,1,0:T(8,128)(2,1)} %get-tuple-element.14) | copy-start | bytes 1572868
  124.7 4.2 %copy-start.9 = (s32[8]{0:T(128)S(1)}, s32[8]{0:T(128)}, u32[]{:S(2)}) copy-start(s32[8]{0:T(128)} %param.18) | copy-start | bytes 100
  127.2 2.3 %copy-start.10 = (s32[8]{0:T(128)S(1)}, s32[8]{0:T(128)}, u32[]{:S(2)}) copy-start(s32[8]{0:T(128)} %param.17) | copy-start | bytes 100
  130.2 2.9 %copy-start.1 = (bf16[2048,384]{1,0:T(8,128)(2,1)S(1)}, bf16[2048,384]{1,0:T(8,128)(2,1)}, u32[]{:S(2)}) copy-start(bf16[2048,384]{1,0:T(8,128)(2,1)} %bitcast_select_fusion.1.wq_ref) | copy-start | bytes 4718596
  130.2 2.9 %copy-start.2 = (bf16[512,512]{1,0:T(8,128)(2,1)S(1)}, bf16[512,512]{1,0:T(8,128)(2,1)}, u32[]{:S(2)}) copy-start(bf16[512,512]{1,0:T(8,128)(2,1)} %bitcast_select_fusion.2.wb_ref) | copy-start | bytes 1572868
  130.2 2.9 %copy-start.3 = (bf16[2,512,256]{2,1,0:T(8,128)(2,1)S(1)}, bf16[2,512,256]{2,1,0:T(8,128)(2,1)}, u32[]{:S(2)}) copy-start(bf16[2,512,256]{2,1,0:T(8,128)(2,1)} %get-tuple-element.29) | copy-start | bytes 1572868
  130.2 2.9 %copy-start.4 = (bf16[2,512,256]{2,1,0:T(8,128)(2,1)S(1)}, bf16[2,512,256]{2,1,0:T(8,128)(2,1)}, u32[]{:S(2)}) copy-start(bf16[2,512,256]{2,1,0:T(8,128)(2,1)} %get-tuple-element.30) | copy-start | bytes 1572868
  130.2 2.9 %copy-start.7 = (f32[2048]{0:T(1024)S(1)}, f32[2048]{0:T(1024)}, u32[]{:S(2)}) copy-start(f32[2048]{0:T(1024)} %param.20) | copy-start | bytes 24580
  130.2 2.9 %copy-start.8 = (f32[512]{0:T(512)S(1)}, f32[512]{0:T(512)}, u32[]{:S(2)}) copy-start(f32[512]{0:T(512)} %param.21) | copy-start | bytes 6148
  170.1 1.3 copy-start.5
